TPU v7x, 512 devices: a whole 4x4x16 slice. The times are simulated.
512 devices in a mesh: blk: 16 (over y_hi, x, core), dom: 32 (over y_lo, z).
Axes of the slice: x: 4, y: 4 (y_hi: 2, y_lo: 2; y = y_hi * 2 + y_lo), z: 16, core: 2. Of those that a mesh axis runs over, the one named last changes fastest.
Arguments:
- nodes: bfloat16 [65536, 512], P(('blk', 'dom')), may hold values from -6 to 6
- experts_list: int32 [512, 4], P(('blk', 'dom')), may hold values from 0 to 15, all different within a row
- w_query: bfloat16 [512, 512], replicated
- w_key: bfloat16 [512, 512], replicated
- w_value: bfloat16 [512, 512], replicated, may hold values from -0.25 to 0.25
- w_out: bfloat16 [512, 512], replicated, may hold values from -0.25 to 0.25
- w_up: bfloat16 [512, 1024], replicated, may hold values from -0.25 to 0.25
- w_down: bfloat16 [1024, 512], replicated, may hold values from -0.1875 to 0.1875
- cotangent: bfloat16 [65536, 512], P(('blk', 'dom')), may hold values from -6 to 6
Outputs:
- layer_out: bfloat16 [65536, 512], P(('blk', 'dom'))
- grad_nodes: bfloat16 [65536, 512], P(('blk', 'dom'))
Inputs may be any that keep to these rules, and one draw needn't show every extreme that they name: `experts_list`: row g names 4 different values; value c stands for the block held at blk index c and the same dom index as block g. Every value is named by some row.
All inputs are finite; a program needn't handle non-finite values.
Results may differ from a plain program's by a relative error of at most 0.0057.
Values may be sent and summed in bfloat16 or wider, within the bound.
A program may use at most 128 MiB of HBM per device.

v0:
```python
import jax
import jax.numpy as jnp
from jax import lax
from jax.sharding import PartitionSpec as P

H = 8
HEAD = 64


EPS = 1e-05
NEG = -1e30


def with_halo(array, sides, width):
    for axis, dim in sides:
        devices, length = (lax.axis_size(axis), array.shape[dim])
        up = [(i, (i + 1) % devices) for i in range(devices)]
        down = [(j, i) for i, j in up]
        last = lax.slice_in_dim(array, length - width, length, axis=dim)
        leading = lax.slice_in_dim(array, 0, width, axis=dim)
        before = lax.ppermute(last, axis, up)
        after = lax.ppermute(leading, axis, down)
        array = jnp.concatenate([before, array, after], axis=dim)
    return array


def shifted(array, axis, by):
    devices = lax.axis_size(axis)
    return lax.ppermute(array, axis, [(i, (i + by) % devices) for i in range(devices)])


def normalize(values):
    mean_v = jnp.mean(values, axis=-1, keepdims=True)
    centered = values - mean_v
    inv_std = lax.rsqrt(jnp.mean(centered * centered, axis=-1, keepdims=True) + EPS)
    return (centered * inv_std, inv_std)


def normalize_back(values, upstream):
    unit, inv_std = normalize(values)
    return inv_std * (
        upstream
        - jnp.mean(upstream, axis=-1, keepdims=True)
        - unit * jnp.mean(upstream * unit, axis=-1, keepdims=True)
    )


def heads_of(rows):
    return rows.reshape(rows.shape[0], H, HEAD)


def attend(queries, keyvals):
    width = queries.shape[1]
    scale = HEAD ** (-0.5)
    qh = heads_of(queries)
    kh = heads_of(keyvals[:, :width])
    vh = heads_of(keyvals[:, width:])
    scores = jnp.einsum("qhd,khd->hqk", qh, kh, preferred_element_type=jnp.float32) * scale
    top = jnp.max(scores, axis=-1, keepdims=True)
    weights = jnp.exp(scores - top)
    total = jnp.sum(weights, axis=-1, keepdims=True)
    mixed = jnp.einsum(
        "hqk,khd->qhd", weights.astype(jnp.bfloat16), vh, preferred_element_type=jnp.float32
    )
    mixed = mixed / jnp.transpose(total, (1, 0, 2))
    lse = (top + jnp.log(total))[..., 0]
    return (mixed.reshape(queries.shape[0], width).astype(jnp.bfloat16), lse)


def attend_back(queries, keyvals, grad_out, lse, delta, qmult):
    width = queries.shape[1]
    scale = HEAD ** (-0.5)
    qh = heads_of(queries)
    kh = heads_of(keyvals[:, :width])
    vh = heads_of(keyvals[:, width:])
    gh = heads_of(grad_out)
    scores = jnp.einsum("qhd,khd->hqk", qh, kh, preferred_element_type=jnp.float32) * scale
    valid = qmult[None, :, None] > 0
    scores = jnp.where(valid, scores, NEG)
    probs = jnp.exp(scores - lse[..., None]) * qmult[None, :, None]
    grad_v = jnp.einsum(
        "hqk,qhd->khd", probs.astype(jnp.bfloat16), gh, preferred_element_type=jnp.float32
    )
    dprob = jnp.einsum("qhd,khd->hqk", gh, vh, preferred_element_type=jnp.float32)
    dscore = (probs * (dprob - delta[..., None]) * scale).astype(jnp.bfloat16)
    grad_q = jnp.einsum("hqk,khd->qhd", dscore, kh, preferred_element_type=jnp.float32)
    grad_k = jnp.einsum("hqk,qhd->khd", dscore, qh, preferred_element_type=jnp.float32)
    count = keyvals.shape[0]
    return (
        grad_q.reshape(queries.shape[0], width),
        jnp.concatenate([grad_k.reshape(count, width), grad_v.reshape(count, width)], 1),
    )


def on_device(nodes, experts_list, w_query, w_key, w_value, w_out, w_up, w_down, cotangent):
    f32 = jnp.float32
    bf16 = jnp.bfloat16
    rows, width = nodes.shape
    groups = lax.axis_size("blk")
    place = lax.axis_index("blk")
    x_full = nodes.astype(f32)
    unit, _ = normalize(x_full)
    normed = unit.astype(bf16)
    queries = jnp.dot(normed, w_query, preferred_element_type=f32).astype(bf16)
    keys = jnp.dot(normed, w_key, preferred_element_type=f32).astype(bf16)
    values = jnp.dot(normed, w_value, preferred_element_type=f32).astype(bf16)
    keyvals = jnp.concatenate([keys, values], 1)
    window = with_halo(keyvals, (("dom", 0),), rows)
    panels = lax.all_gather(keyvals, "blk", axis=0, tiled=True)
    listed = experts_list[0]
    listed_count = listed.shape[0]
    chosen = jnp.take(panels.reshape(groups, rows, 2 * width), listed, axis=0)
    all_keys = jnp.concatenate([window, chosen.reshape(listed_count * rows, 2 * width)], 0)
    mixed, lse = attend(queries, all_keys)
    resid = x_full + jnp.dot(mixed, w_out, preferred_element_type=f32)
    unit2, _ = normalize(resid)
    normed2 = unit2.astype(bf16)
    pre = jnp.dot(normed2, w_up, preferred_element_type=f32)
    act, gelu_back = jax.vjp(jax.nn.gelu, pre)
    layer_out = (resid + jnp.dot(act.astype(bf16), w_down, preferred_element_type=f32)).astype(bf16)
    grad_act = jnp.dot(cotangent, w_down.T, preferred_element_type=f32)
    grad_pre = gelu_back(grad_act)[0].astype(bf16)
    grad_norm2 = jnp.dot(grad_pre, w_up.T, preferred_element_type=f32)
    grad_resid = cotangent.astype(f32) + normalize_back(resid, grad_norm2)
    grad_mixed = jnp.dot(grad_resid.astype(bf16), w_out.T, preferred_element_type=f32).astype(bf16)
    delta = jnp.sum(heads_of(grad_mixed).astype(f32) * heads_of(mixed).astype(f32), axis=-1).T
    ones_rows = jnp.ones((rows,), f32)
    grad_q, grad_kv = attend_back(queries, all_keys, grad_mixed, lse, delta, ones_rows)
    from_upper = shifted(grad_kv[:rows].astype(jnp.bfloat16), "dom", -1).astype(jnp.float32)
    from_lower = shifted(grad_kv[2 * rows : 3 * rows].astype(jnp.bfloat16), "dom", 1).astype(
        jnp.float32
    )
    own_grad = grad_kv[rows : 2 * rows] + from_upper + from_lower
    listed_parts = grad_kv[3 * rows :].reshape(listed_count, rows, 2 * width)
    onehot = (listed[:, None] == jnp.arange(groups, dtype=jnp.int32)[None, :]).astype(f32)
    far_parts = jnp.einsum("eg,erc->grc", onehot, listed_parts).reshape(groups * rows, 2 * width)

    def carry_step(step, running):
        running = shifted(running.astype(jnp.bfloat16), "blk", 1).astype(running.dtype)
        target = (place - step - 1) % groups
        return running + lax.dynamic_slice_in_dim(far_parts, target * rows, rows, 0)

    first = lax.dynamic_slice_in_dim(far_parts, (place - 1) % groups * rows, rows, 0)
    far_grad = lax.fori_loop(1, groups, carry_step, first)
    key_grad = own_grad + far_grad
    grad_in = (
        jnp.dot(grad_q.astype(bf16), w_query.T, preferred_element_type=f32)
        + jnp.dot(key_grad[:, :width].astype(bf16), w_key.T, preferred_element_type=f32)
        + jnp.dot(key_grad[:, width:].astype(bf16), w_value.T, preferred_element_type=f32)
    )
    grad_nodes = (grad_resid + normalize_back(x_full, grad_in)).astype(bf16)
    return (layer_out, grad_nodes)


def solution(mesh):
    return jax.shard_map(
        on_device,
        mesh=mesh,
        in_specs=(
            P(("blk", "dom"), None),
            P(("blk", "dom"), None),
            P(),
            P(),
            P(),
            P(),
            P(),
            P(),
            P(("blk", "dom"), None),
        ),
        out_specs=(P(("blk", "dom"), None), P(("blk", "dom"), None)),
        check_vma=False,
    )
```

profile of v0, /device:TPU:8, one launch (start us, length us, event | category | flops | bytes accessed | tf_op | source)
XLA Modules:
  0.0 364.6 jit_solution(6669680879408683189)
XLA Ops:
  13.0 11.3 %collective-permute-start.2 = (bf16[128,1024]{1,0:T(8,128)(2,1)}, bf16[128,1024]{1,0:T(8,128)(2,1)S(1)}, u32[]{:S(2)}, u32[]{:S(2)}) collective-permute-start(bf16[128,1024]{1,0:T(8,128)(2,1)} %pad_maximum_fusion.2), channel_id=1, source_target_pairs={{1,0},{2,1},{3,2},{4,3},{5,4},{6,5},{7,6},{8,7},{9,8},{10,9},{11,1... | collective-permute-start | bytes 786440 | tf_op jit(solution)/shard_map/ppermute | solution.py:22
  24.3 1.9 collective-permute-start.1
  28.9 1.8 copy.22
  31.8 4.5 %collective-permute-done.1 = bf16[128,1024]{1,0:T(8,128)(2,1)S(1)} collective-permute-done((bf16[128,1024]{1,0:T(8,128)(2,1)}, bf16[128,1024]{1,0:T(8,128)(2,1)S(1)}, u32[]{:S(2)}, u32[]{:S(2)}) %collective-permute-start.1) | collective-permute-done | bytes 262176 | tf_op jit(solution)/shard_map/ppermute | solution.py:21
  37.1 51.1 %all-gather.2.cloned.1.call-done = bf16[2048,1024]{1,0:T(8,128)(2,1)} async-done(((bf16[128,1024]{1,0:T(8,128)(2,1)}), bf16[2048,1024]{1,0:T(8,128)(2,1)}) %all-gather.2.cloned.1.call-update) | async-done | bytes 4194320 | tf_op jit(solution)/shard_map/all_gather | solution.py:109
  88.2 2.8 gather_fusion
  99.1 3.6 fusion.82
  103.9 2.1 convolution_convert_fusion.1
  108.0 3.3 multiply_convert_fusion
  112.1 1.7 fusion.89
  113.8 2.1 fusion.7
  115.9 1.8 copy.26
  117.7 2.8 copy.27
  126.2 4.9 %copy.29 = f32[16,128,1024]{2,1,0:T(8,128)S(1)} copy(f32[16,128,1024]{2,0,1:T(8,128)S(1)} %fusion.5) | data formatting | bytes 16777216 | tf_op jit(solution)/shard_map/eg,erc->grc/dot_general | solution.py:136
  131.1 2.8 fusion.83
  133.9 3.4 collective-permute-start.4
  137.3 5.3 %collective-permute-start.3 = (bf16[128,1024]{1,0:T(8,128)(2,1)}, bf16[128,1024]{1,0:T(8,128)(2,1)}, u32[]{:S(2)}, u32[]{:S(2)}) collective-permute-start(bf16[128,1024]{1,0:T(8,128)(2,1)} %get-tuple-element.127), channel_id=1, source_target_pairs={{0,31},{1,0},{2,1},{3,2},{4,3},{5,4},{6,5},{7,6},{8,7},{9,8},{10,9... | collective-permute-start | bytes 786440 | tf_op jit(solution)/shard_map/ppermute | solution.py:29
  142.7 211.9 %while.15 = (s32[]{:T(128)}, f32[128,1024]{1,0:T(8,128)S(1)}, s32[]{:T(128)}, f32[2048,1024]{1,0:T(8,128)}, s32[]{:T(128)}, /*index=5*/s32[]{:T(128)}, s32[]{:T(...) while((s32[]{:T(128)}, f32[128,1024]{1,0:T(8,128)S(1)}, s32[]{:T(128)}, f32[2048,1024]{1,0:T(8,128)}, ...), condition=%wide.region_10.11_spmd, body=%wide.region_9.10_spmd.sunk | while | flops 393235 | bytes 4194664 | solution.py:144
  143.4 1.9 collective-permute-start
  145.4 9.6 %collective-permute-done = bf16[128,1024]{1,0:T(8,128)(2,1)S(1)} collective-permute-done((bf16[128,1024]{1,0:T(8,128)(2,1)}, bf16[128,1024]{1,0:T(8,128)(2,1)S(1)}, u32[]{:S(2)}, u32[]{:S(2)}) %collective-permute-start) | collective-permute-done | bytes 262176 | tf_op jit(solution)/shard_map/while/body/eval_jaxpr/ppermute | solution.py:29
  157.6 1.9 collective-permute-start
  159.5 9.6 %collective-permute-done = bf16[128,1024]{1,0:T(8,128)(2,1)S(1)} collective-permute-done((bf16[128,1024]{1,0:T(8,128)(2,1)}, bf16[128,1024]{1,0:T(8,128)(2,1)S(1)}, u32[]{:S(2)}, u32[]{:S(2)}) %collective-permute-start) | collective-permute-done | bytes 262176 | tf_op jit(solution)/shard_map/while/body/eval_jaxpr/ppermute | solution.py:29
  171.7 1.9 collective-permute-start
  173.6 9.6 %collective-permute-done = bf16[128,1024]{1,0:T(8,128)(2,1)S(1)} collective-permute-done((bf16[128,1024]{1,0:T(8,128)(2,1)}, bf16[128,1024]{1,0:T(8,128)(2,1)S(1)}, u32[]{:S(2)}, u32[]{:S(2)}) %collective-permute-start) | collective-permute-done | bytes 262176 | tf_op jit(solution)/shard_map/while/body/eval_jaxpr/ppermute | solution.py:29
  185.8 1.9 collective-permute-start
  187.8 9.6 %collective-permute-done = bf16[128,1024]{1,0:T(8,128)(2,1)S(1)} collective-permute-done((bf16[128,1024]{1,0:T(8,128)(2,1)}, bf16[128,1024]{1,0:T(8,128)(2,1)S(1)}, u32[]{:S(2)}, u32[]{:S(2)}) %collective-permute-start) | collective-permute-done | bytes 262176 | tf_op jit(solution)/shard_map/while/body/eval_jaxpr/ppermute | solution.py:29
  199.9 1.9 collective-permute-start
  201.9 9.6 %collective-permute-done = bf16[128,1024]{1,0:T(8,128)(2,1)S(1)} collective-permute-done((bf16[128,1024]{1,0:T(8,128)(2,1)}, bf16[128,1024]{1,0:T(8,128)(2,1)S(1)}, u32[]{:S(2)}, u32[]{:S(2)}) %collective-permute-start) | collective-permute-done | bytes 262176 | tf_op jit(solution)/shard_map/while/body/eval_jaxpr/ppermute | solution.py:29
  214.1 1.9 collective-permute-start
  216.0 9.6 %collective-permute-done = bf16[128,1024]{1,0:T(8,128)(2,1)S(1)} collective-permute-done((bf16[128,1024]{1,0:T(8,128)(2,1)}, bf16[128,1024]{1,0:T(8,128)(2,1)S(1)}, u32[]{:S(2)}, u32[]{:S(2)}) %collective-permute-start) | collective-permute-done | bytes 262176 | tf_op jit(solution)/shard_map/while/body/eval_jaxpr/ppermute | solution.py:29
  228.2 1.9 collective-permute-start
  230.1 9.6 %collective-permute-done = bf16[128,1024]{1,0:T(8,128)(2,1)S(1)} collective-permute-done((bf16[128,1024]{1,0:T(8,128)(2,1)}, bf16[128,1024]{1,0:T(8,128)(2,1)S(1)}, u32[]{:S(2)}, u32[]{:S(2)}) %collective-permute-start) | collective-permute-done | bytes 262176 | tf_op jit(solution)/shard_map/while/body/eval_jaxpr/ppermute | solution.py:29
  242.3 1.9 collective-permute-start
  244.3 9.6 %collective-permute-done = bf16[128,1024]{1,0:T(8,128)(2,1)S(1)} collective-permute-done((bf16[128,1024]{1,0:T(8,128)(2,1)}, bf16[128,1024]{1,0:T(8,128)(2,1)S(1)}, u32[]{:S(2)}, u32[]{:S(2)}) %collective-permute-start) | collective-permute-done | bytes 262176 | tf_op jit(solution)/shard_map/while/body/eval_jaxpr/ppermute | solution.py:29
  256.4 1.9 collective-permute-start
  258.4 9.6 %collective-permute-done = bf16[128,1024]{1,0:T(8,128)(2,1)S(1)} collective-permute-done((bf16[128,1024]{1,0:T(8,128)(2,1)}, bf16[128,1024]{1,0:T(8,128)(2,1)S(1)}, u32[]{:S(2)}, u32[]{:S(2)}) %collective-permute-start) | collective-permute-done | bytes 262176 | tf_op jit(solution)/shard_map/while/body/eval_jaxpr/ppermute | solution.py:29
  270.6 1.9 collective-permute-start
  272.5 9.6 %collective-permute-done = bf16[128,1024]{1,0:T(8,128)(2,1)S(1)} collective-permute-done((bf16[128,1024]{1,0:T(8,128)(2,1)}, bf16[128,1024]{1,0:T(8,128)(2,1)S(1)}, u32[]{:S(2)}, u32[]{:S(2)}) %collective-permute-start) | collective-permute-done | bytes 262176 | tf_op jit(solution)/shard_map/while/body/eval_jaxpr/ppermute | solution.py:29
  284.7 1.9 collective-permute-start
  286.6 9.6 %collective-permute-done = bf16[128,1024]{1,0:T(8,128)(2,1)S(1)} collective-permute-done((bf16[128,1024]{1,0:T(8,128)(2,1)}, bf16[128,1024]{1,0:T(8,128)(2,1)S(1)}, u32[]{:S(2)}, u32[]{:S(2)}) %collective-permute-start) | collective-permute-done | bytes 262176 | tf_op jit(solution)/shard_map/while/body/eval_jaxpr/ppermute | solution.py:29
  298.8 1.9 collective-permute-start
  300.8 9.6 %collective-permute-done = bf16[128,1024]{1,0:T(8,128)(2,1)S(1)} collective-permute-done((bf16[128,1024]{1,0:T(8,128)(2,1)}, bf16[128,1024]{1,0:T(8,128)(2,1)S(1)}, u32[]{:S(2)}, u32[]{:S(2)}) %collective-permute-start) | collective-permute-done | bytes 262176 | tf_op jit(solution)/shard_map/while/body/eval_jaxpr/ppermute | solution.py:29
  312.9 1.9 collective-permute-start
  314.9 9.6 %collective-permute-done = bf16[128,1024]{1,0:T(8,128)(2,1)S(1)} collective-permute-done((bf16[128,1024]{1,0:T(8,128)(2,1)}, bf16[128,1024]{1,0:T(8,128)(2,1)S(1)}, u32[]{:S(2)}, u32[]{:S(2)}) %collective-permute-start) | collective-permute-done | bytes 262176 | tf_op jit(solution)/shard_map/while/body/eval_jaxpr/ppermute | solution.py:29
  327.1 1.9 collective-permute-start
  329.0 9.6 %collective-permute-done = bf16[128,1024]{1,0:T(8,128)(2,1)S(1)} collective-permute-done((bf16[128,1024]{1,0:T(8,128)(2,1)}, bf16[128,1024]{1,0:T(8,128)(2,1)S(1)}, u32[]{:S(2)}, u32[]{:S(2)}) %collective-permute-start) | collective-permute-done | bytes 262176 | tf_op jit(solution)/shard_map/while/body/eval_jaxpr/ppermute | solution.py:29
  341.2 1.9 collective-permute-start
  343.1 9.6 %collective-permute-done = bf16[128,1024]{1,0:T(8,128)(2,1)S(1)} collective-permute-done((bf16[128,1024]{1,0:T(8,128)(2,1)}, bf16[128,1024]{1,0:T(8,128)(2,1)S(1)}, u32[]{:S(2)}, u32[]{:S(2)}) %collective-permute-start) | collective-permute-done | bytes 262176 | tf_op jit(solution)/shard_map/while/body/eval_jaxpr/ppermute | solution.py:29
  (161 shorter events, 69.9 us)
Async XLA Ops:
  7.2 89.8 %copy-start = (bf16[512,1024]{1,0:T(8,128)(2,1)S(1)}, bf16[512,1024]{1,0:T(8,128)(2,1)}, u32[]{:S(2)}) copy-start(bf16[512,1024]{1,0:T(8,128)(2,1)} %param.17) | copy-start | bytes 3145732
  7.2 81.0 %all-gather.2.cloned.1.call-start = ((), (), s32[]{:S(2)}) async-start(), calls=%async_computation | async-start | bytes 4456448 | tf_op jit(solution)/shard_map/all_gather | solution.py:109
  13.0 18.0 %collective-permute-start.2 = (bf16[128,1024]{1,0:T(8,128)(2,1)}, bf16[128,1024]{1,0:T(8,128)(2,1)S(1)}, u32[]{:S(2)}, u32[]{:S(2)}) collective-permute-start(bf16[128,1024]{1,0:T(8,128)(2,1)} %pad_maximum_fusion.2), channel_id=1, source_target_pairs={{1,0},{2,1},{3,2},{4,3},{5,4},{6,5},{7,6},{8,7},{9,8},{10,9},{11,1... | collective-permute-start | bytes 786440 | tf_op jit(solution)/shard_map/ppermute | solution.py:22
  24.3 12.0 %collective-permute-start.1 = (bf16[128,1024]{1,0:T(8,128)(2,1)}, bf16[128,1024]{1,0:T(8,128)(2,1)S(1)}, u32[]{:S(2)}, u32[]{:S(2)}) collective-permute-start(bf16[128,1024]{1,0:T(8,128)(2,1)} %pad_maximum_fusion.2), channel_id=1, source_target_pairs={{0,1},{1,2},{2,3},{3,4},{4,5},{5,6},{6,7},{7,8},{8,9},{9,10},{10,1... | collective-permute-start | bytes 786440 | tf_op jit(solution)/shard_map/ppermute | solution.py:21
  93.9 1.8 copy-start.1
  93.9 1.9 copy-start.5
  94.0 1.9 copy-start.11
  94.8 3.3 copy-start.26
  95.8 3.3 copy-start.16
  96.2 7.2 %copy-start.7 = (f32[128,512]{1,0:T(8,128)}, f32[128,512]{1,0:T(8,128)S(1)}, u32[]{:S(2)}) copy-start(f32[128,512]{1,0:T(8,128)S(1)} %get-tuple-element.134) | copy-start | bytes 786436
  97.3 0.8 copy-start.15
  111.2 2.5 copy-start.2
  120.5 1.8 copy-start.3
  122.3 1.5 copy-start.9
  122.3 2.5 copy-start.25
  131.1 11.6 %copy-start.4 = (f32[16,128,1024]{2,1,0:T(8,128)}, f32[16,128,1024]{2,1,0:T(8,128)S(1)}, u32[]{:S(2)}) copy-start(f32[16,128,1024]{2,1,0:T(8,128)S(1)} %copy.29) | copy-start | bytes 25165828
  133.9 220.7 %collective-permute-start.4 = (bf16[128,1024]{1,0:T(8,128)(2,1)}, bf16[128,1024]{1,0:T(8,128)(2,1)}, u32[]{:S(2)}, u32[]{:S(2)}) collective-permute-start(bf16[128,1024]{1,0:T(8,128)(2,1)} %get-tuple-element.128), channel_id=1, source_target_pairs={{0,1},{1,2},{2,3},{3,4},{4,5},{5,6},{6,7},{7,8},{8,9},{9,10},{10,1... | collective-permute-start | bytes 786440 | tf_op jit(solution)/shard_map/ppermute | solution.py:29
  137.3 217.3 %collective-permute-start.3 = (bf16[128,1024]{1,0:T(8,128)(2,1)}, bf16[128,1024]{1,0:T(8,128)(2,1)}, u32[]{:S(2)}, u32[]{:S(2)}) collective-permute-start(bf16[128,1024]{1,0:T(8,128)(2,1)} %get-tuple-element.127), channel_id=1, source_target_pairs={{0,31},{1,0},{2,1},{3,2},{4,3},{5,4},{6,5},{7,6},{8,7},{9,8},{10,9... | collective-permute-start | bytes 786440 | tf_op jit(solution)/shard_map/ppermute | solution.py:29
  143.4 11.5 %collective-permute-start = (bf16[128,1024]{1,0:T(8,128)(2,1)}, bf16[128,1024]{1,0:T(8,128)(2,1)S(1)}, u32[]{:S(2)}, u32[]{:S(2)}) collective-permute-start(bf16[128,1024]{1,0:T(8,128)(2,1)} %convert_element_type.201), channel_id=1, source_target_pairs={{0,32},{32,64},{64,96},{96,128},{128,160},{160,192},{192,224},{224... | collective-permute-start | bytes 786440 | tf_op jit(solution)/shard_map/while/body/eval_jaxpr/ppermute | solution.py:29
  155.0 0.7 copy-start.6
  157.6 11.5 %collective-permute-start = (bf16[128,1024]{1,0:T(8,128)(2,1)}, bf16[128,1024]{1,0:T(8,128)(2,1)S(1)}, u32[]{:S(2)}, u32[]{:S(2)}) collective-permute-start(bf16[128,1024]{1,0:T(8,128)(2,1)} %convert_element_type.201), channel_id=1, source_target_pairs={{0,32},{32,64},{64,96},{96,128},{128,160},{160,192},{192,224},{224... | collective-permute-start | bytes 786440 | tf_op jit(solution)/shard_map/while/body/eval_jaxpr/ppermute | solution.py:29
  169.1 0.7 copy-start.6
  171.7 11.5 %collective-permute-start = (bf16[128,1024]{1,0:T(8,128)(2,1)}, bf16[128,1024]{1,0:T(8,128)(2,1)S(1)}, u32[]{:S(2)}, u32[]{:S(2)}) collective-permute-start(bf16[128,1024]{1,0:T(8,128)(2,1)} %convert_element_type.201), channel_id=1, source_target_pairs={{0,32},{32,64},{64,96},{96,128},{128,160},{160,192},{192,224},{224... | collective-permute-start | bytes 786440 | tf_op jit(solution)/shard_map/while/body/eval_jaxpr/ppermute | solution.py:29
  183.2 0.7 copy-start.6
  185.8 11.5 %collective-permute-start = (bf16[128,1024]{1,0:T(8,128)(2,1)}, bf16[128,1024]{1,0:T(8,128)(2,1)S(1)}, u32[]{:S(2)}, u32[]{:S(2)}) collective-permute-start(bf16[128,1024]{1,0:T(8,128)(2,1)} %convert_element_type.201), channel_id=1, source_target_pairs={{0,32},{32,64},{64,96},{96,128},{128,160},{160,192},{192,224},{224... | collective-permute-start | bytes 786440 | tf_op jit(solution)/shard_map/while/body/eval_jaxpr/ppermute | solution.py:29
  197.3 0.7 copy-start.6
  199.9 11.5 %collective-permute-start = (bf16[128,1024]{1,0:T(8,128)(2,1)}, bf16[128,1024]{1,0:T(8,128)(2,1)S(1)}, u32[]{:S(2)}, u32[]{:S(2)}) collective-permute-start(bf16[128,1024]{1,0:T(8,128)(2,1)} %convert_element_type.201), channel_id=1, source_target_pairs={{0,32},{32,64},{64,96},{96,128},{128,160},{160,192},{192,224},{224... | collective-permute-start | bytes 786440 | tf_op jit(solution)/shard_map/while/body/eval_jaxpr/ppermute | solution.py:29
  211.4 0.7 copy-start.6
  214.1 11.5 %collective-permute-start = (bf16[128,1024]{1,0:T(8,128)(2,1)}, bf16[128,1024]{1,0:T(8,128)(2,1)S(1)}, u32[]{:S(2)}, u32[]{:S(2)}) collective-permute-start(bf16[128,1024]{1,0:T(8,128)(2,1)} %convert_element_type.201), channel_id=1, source_target_pairs={{0,32},{32,64},{64,96},{96,128},{128,160},{160,192},{192,224},{224... | collective-permute-start | bytes 786440 | tf_op jit(solution)/shard_map/while/body/eval_jaxpr/ppermute | solution.py:29
  225.6 0.7 copy-start.6
  228.2 11.5 %collective-permute-start = (bf16[128,1024]{1,0:T(8,128)(2,1)}, bf16[128,1024]{1,0:T(8,128)(2,1)S(1)}, u32[]{:S(2)}, u32[]{:S(2)}) collective-permute-start(bf16[128,1024]{1,0:T(8,128)(2,1)} %convert_element_type.201), channel_id=1, source_target_pairs={{0,32},{32,64},{64,96},{96,128},{128,160},{160,192},{192,224},{224... | collective-permute-start | bytes 786440 | tf_op jit(solution)/shard_map/while/body/eval_jaxpr/ppermute | solution.py:29
  242.3 11.5 %collective-permute-start = (bf16[128,1024]{1,0:T(8,128)(2,1)}, bf16[128,1024]{1,0:T(8,128)(2,1)S(1)}, u32[]{:S(2)}, u32[]{:S(2)}) collective-permute-start(bf16[128,1024]{1,0:T(8,128)(2,1)} %convert_element_type.201), channel_id=1, source_target_pairs={{0,32},{32,64},{64,96},{96,128},{128,160},{160,192},{192,224},{224... | collective-permute-start | bytes 786440 | tf_op jit(solution)/shard_map/while/body/eval_jaxpr/ppermute | solution.py:29
  256.4 11.5 %collective-permute-start = (bf16[128,1024]{1,0:T(8,128)(2,1)}, bf16[128,1024]{1,0:T(8,128)(2,1)S(1)}, u32[]{:S(2)}, u32[]{:S(2)}) collective-permute-start(bf16[128,1024]{1,0:T(8,128)(2,1)} %convert_element_type.201), channel_id=1, source_target_pairs={{0,32},{32,64},{64,96},{96,128},{128,160},{160,192},{192,224},{224... | collective-permute-start | bytes 786440 | tf_op jit(solution)/shard_map/while/body/eval_jaxpr/ppermute | solution.py:29
  270.6 11.5 %collective-permute-start = (bf16[128,1024]{1,0:T(8,128)(2,1)}, bf16[128,1024]{1,0:T(8,128)(2,1)S(1)}, u32[]{:S(2)}, u32[]{:S(2)}) collective-permute-start(bf16[128,1024]{1,0:T(8,128)(2,1)} %convert_element_type.201), channel_id=1, source_target_pairs={{0,32},{32,64},{64,96},{96,128},{128,160},{160,192},{192,224},{224... | collective-permute-start | bytes 786440 | tf_op jit(solution)/shard_map/while/body/eval_jaxpr/ppermute | solution.py:29
  284.7 11.5 %collective-permute-start = (bf16[128,1024]{1,0:T(8,128)(2,1)}, bf16[128,1024]{1,0:T(8,128)(2,1)S(1)}, u32[]{:S(2)}, u32[]{:S(2)}) collective-permute-start(bf16[128,1024]{1,0:T(8,128)(2,1)} %convert_element_type.201), channel_id=1, source_target_pairs={{0,32},{32,64},{64,96},{96,128},{128,160},{160,192},{192,224},{224... | collective-permute-start | bytes 786440 | tf_op jit(solution)/shard_map/while/body/eval_jaxpr/ppermute | solution.py:29
  298.8 11.5 %collective-permute-start = (bf16[128,1024]{1,0:T(8,128)(2,1)}, bf16[128,1024]{1,0:T(8,128)(2,1)S(1)}, u32[]{:S(2)}, u32[]{:S(2)}) collective-permute-start(bf16[128,1024]{1,0:T(8,128)(2,1)} %convert_element_type.201), channel_id=1, source_target_pairs={{0,32},{32,64},{64,96},{96,128},{128,160},{160,192},{192,224},{224... | collective-permute-start | bytes 786440 | tf_op jit(solution)/shard_map/while/body/eval_jaxpr/ppermute | solution.py:29
  312.9 11.5 %collective-permute-start = (bf16[128,1024]{1,0:T(8,128)(2,1)}, bf16[128,1024]{1,0:T(8,128)(2,1)S(1)}, u32[]{:S(2)}, u32[]{:S(2)}) collective-permute-start(bf16[128,1024]{1,0:T(8,128)(2,1)} %convert_element_type.201), channel_id=1, source_target_pairs={{0,32},{32,64},{64,96},{96,128},{128,160},{160,192},{192,224},{224... | collective-permute-start | bytes 786440 | tf_op jit(solution)/shard_map/while/body/eval_jaxpr/ppermute | solution.py:29
  327.1 11.5 %collective-permute-start = (bf16[128,1024]{1,0:T(8,128)(2,1)}, bf16[128,1024]{1,0:T(8,128)(2,1)S(1)}, u32[]{:S(2)}, u32[]{:S(2)}) collective-permute-start(bf16[128,1024]{1,0:T(8,128)(2,1)} %convert_element_type.201), channel_id=1, source_target_pairs={{0,32},{32,64},{64,96},{96,128},{128,160},{160,192},{192,224},{224... | collective-permute-start | bytes 786440 | tf_op jit(solution)/shard_map/while/body/eval_jaxpr/ppermute | solution.py:29
  341.2 11.5 %collective-permute-start = (bf16[128,1024]{1,0:T(8,128)(2,1)}, bf16[128,1024]{1,0:T(8,128)(2,1)S(1)}, u32[]{:S(2)}, u32[]{:S(2)}) collective-permute-start(bf16[128,1024]{1,0:T(8,128)(2,1)} %convert_element_type.201), channel_id=1, source_target_pairs={{0,32},{32,64},{64,96},{96,128},{128,160},{160,192},{192,224},{224... | collective-permute-start | bytes 786440 | tf_op jit(solution)/shard_map/while/body/eval_jaxpr/ppermute | solution.py:29
  354.6 1.5 copy-start.12
  354.6 1.5 copy-start.14
  354.6 1.8 copy-start.10
  354.6 2.2 copy-start.8
  354.6 2.2 copy-start.13
  354.6 2.2 copy-start.17
  354.7 2.2 copy-start.20
  354.7 2.2 copy-start.22
  354.7 2.2 copy-start.24
  (13 other events, 8.5 us)
Sparse Core Ops, SparseCore 0:
  13.1 75.0 all-gather.1
where the time goes:
time: 366 us; the launch traced here: 365 us
  waiting for transfers between devices  199 us (54%)
  starting transfers between devices  50.6 us (14%)
  other arithmetic  41.9 us (11%)
  local copies, waits for them, and re-layouts  33.2 us (9%)
  matrix products  24.4 us (7%)
  between operations  14.6 us (4%)
    ppermute x17, waiting for transfers between devices, shifted(): lax.ppermute(array, axis, [(i, (i + by) % devices) for i in range(devices)])  143 us
    all_gather x1, waiting for transfers between devices, on_device(): panels = lax.all_gather(keyvals, 'blk', axis=0, tiled=True)  51.1 us
    ppermute x17, starting transfers between devices, shifted(): lax.ppermute(array, axis, [(i, (i + by) % devices) for i in range(devices)])  37.4 us
    add x15, other arithmetic, carry_step(): return running + lax.dynamic_slice_in_dim(far_parts, target * rows, rows, 0)  17.4 us
    ppermute x1, starting transfers between devices, with_halo(): after = lax.ppermute(leading, axis, down)  11.3 us
    convert_element_type x15, other arithmetic, carry_step(): running.astype(jnp.bfloat16)  11.1 us
    while x30, local copies, waits for them, and re-layouts  10.5 us
  transfers between devices with their start and end apart: 20, of which 17 were waited for; matrix products, arithmetic and copies ran while one was open for 10% of the time, Pallas kernels for 0%

commit v1 on v0

v1 whole, which is shorter than its diff:
```python
import functools

import jax
import jax.numpy as jnp
from jax import lax
from jax.experimental import pallas as pl
from jax.experimental.pallas import tpu as pltpu
from jax.sharding import PartitionSpec as P

EPS = 1e-05
MESH = pl.DeviceIdType.MESH
D = 512
FF = 1024
ROWS = 128
HALF = 64
DHALF = 256
PAIRS = 4
F32 = jnp.float32
BF16 = jnp.bfloat16


def normalize(values):
    mean_v = jnp.mean(values, axis=-1, keepdims=True)
    centered = values - mean_v
    inv_std = lax.rsqrt(jnp.mean(centered * centered, axis=-1, keepdims=True) + EPS)
    return (centered * inv_std, inv_std)


def normalize_back(unit, inv_std, upstream):
    return inv_std * (
        upstream
        - jnp.mean(upstream, axis=-1, keepdims=True)
        - unit * jnp.mean(upstream * unit, axis=-1, keepdims=True)
    )


def dot(a, b):
    return jnp.dot(a, b, preferred_element_type=F32)


def dot_t(a, b):
    return lax.dot_general(a, b, (((1,), (1,)), ((), ())), preferred_element_type=F32)


def head_stack(tile):
    low = lax.broadcasted_iota(jnp.int32, tile.shape, 1) < 64
    zero = jnp.zeros_like(tile)
    return jnp.concatenate([jnp.where(low, tile, zero), jnp.where(low, zero, tile)], 0)


def head_join(stacked):
    low = lax.broadcasted_iota(jnp.int32, (ROWS, 128), 1) < 64
    return jnp.where(low, stacked[:ROWS], stacked[ROWS:])


def kernel(
    listed,
    nodes_hbm,
    list_hbm,
    wq_hbm,
    wk_hbm,
    wv_hbm,
    wo_hbm,
    wu_hbm,
    wd_hbm,
    cot_hbm,
    out_hbm,
    gout_hbm,
    xv,
    cotv,
    wq,
    wkv,
    wo,
    wu,
    wd,
    gath,
    halo,
    kv,
    q2,
    q2t,
    g2,
    g2t,
    wexp,
    mstat,
    lstat,
    oacc,
    fstat,
    mixv,
    delt,
    dq,
    dt,
    part,
    psib,
    lsib,
    hsend,
    hrecv,
    xo,
    yl,
    yr,
    sbuf,
    tbuf,
    ybuf,
    outv,
    goutv,
    lsem,
    gsend,
    grecv,
    rsend,
    rrecv,
):
    blk = lax.axis_index("blk")
    dom = lax.axis_index("dom")
    ndom = lax.axis_size("dom")
    core = blk % 2
    x = (blk // 2) % 4
    h = blk // 8

    def at(xx, hh, cc):
        return hh * 8 + (xx % 4) * 2 + cc

    right = {"blk": at(x + 1, h, core), "dom": dom}
    left = {"blk": at(x + 3, h, core), "dom": dom}
    across = {"blk": at(x, 1 - h, core), "dom": dom}
    twin = {"blk": at(x, h, 1 - core), "dom": dom}
    up = {"blk": blk, "dom": (dom + 1) % ndom}
    down = {"blk": blk, "dom": (dom + ndom - 1) % ndom}

    loads = []

    def load(src, dst):
        copy = pltpu.make_async_copy(src, dst, lsem.at[len(loads)])
        copy.start()
        loads.append(copy)
        return copy

    ld_x = load(nodes_hbm, xv)
    ld_wk = load(wk_hbm, wkv.at[:, pl.ds(0, D)])
    ld_wv = load(wv_hbm, wkv.at[:, pl.ds(D, D)])
    ld_wq = load(wq_hbm, wq)
    ld_wo = load(wo_hbm, wo)
    ld_wu = load(wu_hbm, wu)
    ld_wd = load(wd_hbm, wd)
    ld_cot = load(cot_hbm, cotv)

    barrier = pltpu.get_barrier_semaphore()
    for peer in (right, left, across, twin, up, down):
        pl.semaphore_signal(barrier, inc=1, device_id=peer, device_id_type=MESH)
    pl.semaphore_wait(barrier, 6)

    sends = []

    def push(src, dst, ssems, rsems, slot, peer):
        copy = pltpu.make_async_remote_copy(
            src_ref=src,
            dst_ref=dst,
            send_sem=ssems.at[slot],
            recv_sem=rsems.at[slot],
            device_id=peer,
            device_id_type=MESH,
        )
        copy.start()
        sends.append(copy)
        return copy

    top = pl.ds(0, HALF)
    bottom = pl.ds(HALF, HALF)
    halves = (top, bottom)

    def block(xx, rr):
        return at(xx, rr, core)

    rows_of = (h, 1 - h)

    own = block(x, h)
    c_r = {}
    c_l = {}
    c_r[0, 0] = push(nodes_hbm.at[top], gath.at[own, top], gsend, grecv, 0, right)
    c_l[0, 1] = push(nodes_hbm.at[bottom], gath.at[own, bottom], gsend, grecv, 5, left)
    c_y = [None, None]
    c_y[0] = push(nodes_hbm.at[top], gath.at[own, top], gsend, grecv, 12, across)
    c_y[1] = push(nodes_hbm.at[bottom], gath.at[own, bottom], gsend, grecv, 13, across)
    c_r[0, 1] = push(nodes_hbm.at[bottom], gath.at[own, bottom], gsend, grecv, 1, right)
    c_l[0, 0] = push(nodes_hbm.at[top], gath.at[own, top], gsend, grecv, 4, left)
    c_up = push(nodes_hbm, halo.at[0], gsend, grecv, 14, up)
    c_dn = push(nodes_hbm, halo.at[1], gsend, grecv, 15, down)
    c_list = push(list_hbm, lsib, gsend, grecv, 24, twin)
    c_tw = []
    c_tw.append(push(nodes_hbm, gath.at[own], gsend, grecv, 16, twin))

    ld_x.wait()
    own_copy = pltpu.make_async_copy(xv, gath.at[own], lsem.at[len(loads)])
    own_copy.start()

    x_full = xv[...].astype(F32)
    unit, inv_std = normalize(x_full)
    normed = unit.astype(BF16)
    ld_wk.wait()
    ld_wv.wait()
    kv[pl.ds(ROWS, ROWS), :] = dot(normed, wkv[...]).astype(BF16)
    ld_wq.wait()
    queries = dot(normed, wq[...]).astype(BF16) * jnp.asarray(0.125, BF16)
    for hp in range(PAIRS):
        stacked = head_stack(queries[:, hp * 128 : (hp + 1) * 128])
        q2[hp] = stacked
        q2t[hp] = jnp.transpose(stacked)

    fwd_r = [None, None]
    fwd_l = [None, None]

    def forward(rr):
        row = rows_of[rr]
        c_r[rr, 0].wait_recv()
        from_left = block(x + 3, row)
        fwd_r[rr] = push(gath.at[from_left, top], gath.at[from_left, top], gsend, grecv, 8 + rr, right)
        c_l[rr, 1].wait_recv()
        from_right = block(x + 1, row)
        fwd_l[rr] = push(
            gath.at[from_right, bottom], gath.at[from_right, bottom], gsend, grecv, 10 + rr, left
        )

    def to_twin(slot, who):
        c_tw.append(push(gath.at[who], gath.at[who], gsend, grecv, slot, twin))

    forward(0)
    other = block(x, 1 - h)
    c_y[0].wait_recv()
    c_r[1, 0] = push(gath.at[other, top], gath.at[other, top], gsend, grecv, 2, right)
    c_l[1, 0] = push(gath.at[other, top], gath.at[other, top], gsend, grecv, 6, left)
    c_y[1].wait_recv()
    c_l[1, 1] = push(gath.at[other, bottom], gath.at[other, bottom], gsend, grecv, 7, left)
    c_r[1, 1] = push(gath.at[other, bottom], gath.at[other, bottom], gsend, grecv, 3, right)
    to_twin(17, other)
    c_r[0, 1].wait_recv()
    to_twin(18, block(x + 3, h))
    c_l[0, 0].wait_recv()
    to_twin(19, block(x + 1, h))

    def project(raw, row0):
        unit_o, _ = normalize(raw.astype(F32))
        kv[pl.ds(row0, ROWS), :] = dot(unit_o.astype(BF16), wkv[...]).astype(BF16)

    def attend(base, count, which):
        for hp in range(PAIRS):
            k = kv[base : base + count, hp * 128 : (hp + 1) * 128]
            v = kv[base : base + count, D + hp * 128 : D + (hp + 1) * 128]
            s = dot_t(q2[hp], k)
            m = jnp.max(s, axis=1, keepdims=True)
            w = jnp.exp(s - m)
            wexp[hp, :, base : base + count] = w
            total = jnp.sum(w, axis=1, keepdims=True)
            oacc[which, hp] = dot(w.astype(BF16), v)
            mstat[which, hp] = jnp.broadcast_to(m, (2 * ROWS, 128))
            lstat[which, hp] = jnp.broadcast_to(total, (2 * ROWS, 128))

    c_up.wait_recv()
    project(halo[0], 0)
    c_dn.wait_recv()
    project(halo[1], 2 * ROWS)
    forward(1)
    attend(0, 3 * ROWS, 0)

    for rr in (0, 1):
        if rr == 1:
            c_r[1, 1].wait_recv()
            to_twin(20, block(x + 3, 1 - h))
            c_l[1, 0].wait_recv()
            to_twin(21, block(x + 1, 1 - h))
        fwd_r[rr].wait_recv()
        fwd_l[rr].wait_recv()
        to_twin(22 + rr, block(x + 2, rows_of[rr]))
    for copy in c_tw:
        copy.wait_recv()
    c_list.wait_recv()
    own_copy.wait()

    for e in range(4):
        project(gath[listed[0, e]], (3 + e) * ROWS)
    attend(3 * ROWS, 4 * ROWS, 1)

    for hp in range(PAIRS):
        m0, m1 = mstat[0, hp], mstat[1, hp]
        m = jnp.maximum(m0, m1)
        a0, a1 = jnp.exp(m0 - m), jnp.exp(m1 - m)
        inv = 1.0 / (a0 * lstat[0, hp] + a1 * lstat[1, hp])
        f0, f1 = a0 * inv, a1 * inv
        fstat[0, hp] = f0
        fstat[1, hp] = f1
        o = oacc[0, hp] * f0 + oacc[1, hp] * f1
        mixv[:, hp * 128 : (hp + 1) * 128] = head_join(o).astype(BF16)

    ld_wo.wait()
    mixed = mixv[...]
    resid = xv[...].astype(F32) + dot(mixed, wo[...])
    unit2, inv_std2 = normalize(resid)
    ld_wu.wait()
    pre = dot(unit2.astype(BF16), wu[...])
    ld_wd.wait()
    ld_cot.wait()
    cot = cotv[...]
    grad_act = dot_t(cot, wd[...])
    c0 = 0.7978845608028654
    sq = pre * pre
    th = jnp.tanh(c0 * (pre + 0.044715 * (sq * pre)))
    act = 0.5 * pre * (1.0 + th)
    slope = 0.5 * (1.0 + th) + 0.5 * pre * (1.0 - th * th) * (c0 * (1.0 + 3.0 * 0.044715 * sq))
    outv[...] = (resid + dot(act.astype(BF16), wd[...])).astype(BF16)
    st_out = pltpu.make_async_copy(outv, out_hbm, lsem.at[len(loads) + 1])
    st_out.start()
    grad_pre = (grad_act * slope).astype(BF16)
    grad_norm2 = dot_t(grad_pre, wu[...])
    grad_resid = cot.astype(F32) + normalize_back(unit2, inv_std2, grad_norm2)
    grad_mixed = dot_t(grad_resid.astype(BF16), wo[...]).astype(BF16)
    for hp in range(PAIRS):
        stacked = head_stack(grad_mixed[:, hp * 128 : (hp + 1) * 128])
        g2[hp] = stacked
        g2t[hp] = jnp.transpose(stacked)
        mixed_pair = mixed[:, hp * 128 : (hp + 1) * 128].astype(F32)
        both = jnp.concatenate([mixed_pair, mixed_pair], 0)
        d = jnp.sum(stacked.astype(F32) * both, axis=1, keepdims=True)
        delt[hp] = jnp.broadcast_to(d, (2 * ROWS, 128))

    def attend_back(base, count, which):
        for hp in range(PAIRS):
            k = kv[base : base + count, hp * 128 : (hp + 1) * 128]
            v = kv[base : base + count, D + hp * 128 : D + (hp + 1) * 128]
            p = wexp[hp, :, base : base + count] * fstat[which, hp][:, :1]
            dp = dot_t(g2[hp], v)
            ds = (p * (dp - delt[hp][:, :1])).astype(BF16)
            dt[hp * 128 : (hp + 1) * 128, base : base + count] = dot(q2t[hp], ds).astype(BF16)
            dt[D + hp * 128 : D + (hp + 1) * 128, base : base + count] = dot(
                g2t[hp], p.astype(BF16)
            ).astype(BF16)
            dq_part = dot(ds, k)
            dq[which, hp] = dq_part

    attend_back(3 * ROWS, 4 * ROWS, 1)

    zero_block = jnp.zeros((D, ROWS), BF16)
    part[4] = zero_block
    psib[4] = zero_block
    c_ps = []
    for e in range(4):
        cols = slice((3 + e) * ROWS, (4 + e) * ROWS)
        part[e] = dot(wkv[...], dt[:, cols]).astype(BF16)
        c_ps.append(push(part.at[e], psib.at[e], rsend, rrecv, e, twin))

    attend_back(0, 3 * ROWS, 0)
    hsend[0] = dot(wkv[...], dt[:, 0:ROWS]).astype(BF16)
    c_hd = push(hsend.at[0], hrecv.at[0], rsend, rrecv, 4, down)
    hsend[1] = dot(wkv[...], dt[:, 2 * ROWS : 3 * ROWS]).astype(BF16)
    c_hu = push(hsend.at[1], hrecv.at[1], rsend, rrecv, 5, up)

    for copy in c_ps:
        copy.wait_recv()

    def slot_of(lists, target):
        slot = jnp.int32(4)
        for e in range(4):
            slot = jnp.where(lists[0, e] == target, jnp.int32(e), slot)
        return slot

    def summed(xx, rr, cols):
        target = block(xx, rows_of[rr])
        return (
            part[slot_of(listed, target), cols, :].astype(F32)
            + psib[slot_of(lsib, target), cols, :].astype(F32)
        )

    da = pl.ds(0, DHALF)
    db = pl.ds(DHALF, DHALF)

    c_x = {}
    for rr in (1, 0):
        s0 = 8 + 6 * rr
        sbuf[rr, 0] = summed(x + 2, rr, da).astype(BF16)
        c_x[rr, 0] = push(sbuf.at[rr, 0], xo.at[rr, 0], rsend, rrecv, s0, right)
        sbuf[rr, 1] = summed(x + 2, rr, db).astype(BF16)
        c_x[rr, 1] = push(sbuf.at[rr, 1], xo.at[rr, 1], rsend, rrecv, s0 + 1, left)
        sbuf[rr, 2] = summed(x + 1, rr, db).astype(BF16)
        c_x[rr, 2] = push(sbuf.at[rr, 2], yl.at[rr, db], rsend, rrecv, s0 + 2, right)
        sbuf[rr, 3] = summed(x + 3, rr, da).astype(BF16)
        c_x[rr, 3] = push(sbuf.at[rr, 3], yr.at[rr, da], rsend, rrecv, s0 + 3, left)
    for rr in (1, 0):
        s0 = 8 + 6 * rr
        c_x[rr, 0].wait_recv()
        sbuf[rr, 4] = (summed(x + 1, rr, da) + xo[rr, 0].astype(F32)).astype(BF16)
        c_x[rr, 4] = push(sbuf.at[rr, 4], yl.at[rr, da], rsend, rrecv, s0 + 4, right)
        c_x[rr, 1].wait_recv()
        sbuf[rr, 5] = (summed(x + 3, rr, db) + xo[rr, 1].astype(F32)).astype(BF16)
        c_x[rr, 5] = push(sbuf.at[rr, 5], yr.at[rr, db], rsend, rrecv, s0 + 5, left)

    own_t = dot(wkv[...], dt[:, ROWS : 2 * ROWS])
    grad_q = jnp.concatenate([head_join(dq[0, hp] + dq[1, hp]) for hp in range(PAIRS)], 1)
    grad_in = dot_t((grad_q * 0.125).astype(BF16), wq[...])

    for slot in (2, 3, 4, 5):
        c_x[1, slot].wait_recv()
    for i, cols in enumerate((da, db)):
        tbuf[i] = (
            summed(x, 1, cols) + yl[1, cols, :].astype(F32) + yr[1, cols, :].astype(F32)
        ).astype(BF16)
        c_x[2, i] = push(tbuf.at[i], ybuf.at[i], rsend, rrecv, 6 + i, across)
    c_hd.wait_recv()
    c_hu.wait_recv()
    own_t = own_t + hrecv[0].astype(F32) + hrecv[1].astype(F32)
    for slot in (2, 3, 4, 5):
        c_x[0, slot].wait_recv()
    own_t = own_t + yl[0].astype(F32) + yr[0].astype(F32)
    own_t = own_t + jnp.concatenate([summed(x, 0, da), summed(x, 0, db)], 0)
    c_x[2, 0].wait_recv()
    c_x[2, 1].wait_recv()
    own_t = own_t + jnp.concatenate([ybuf[0], ybuf[1]], 0).astype(F32)
    grad_in = grad_in + jnp.transpose(own_t)
    unit_b, inv_b = normalize(xv[...].astype(F32))
    goutv[...] = (grad_resid + normalize_back(unit_b, inv_b, grad_in)).astype(BF16)
    st_gout = pltpu.make_async_copy(goutv, gout_hbm, lsem.at[len(loads) + 2])
    st_gout.start()
    for copy in sends:
        copy.wait_send()
    st_out.wait()
    st_gout.wait()


def on_device(nodes, experts_list, w_query, w_key, w_value, w_out, w_up, w_down, cotangent):
    rows, width = nodes.shape
    hbm = pl.BlockSpec(memory_space=pl.ANY)
    tile = lambda *shape, dtype=BF16: pltpu.VMEM(shape, dtype)
    out = jax.ShapeDtypeStruct((rows, width), BF16)
    return pl.pallas_call(
        kernel,
        out_shape=(out, out),
        in_specs=[pl.BlockSpec(memory_space=pltpu.SMEM)] + [hbm] * 9,
        out_specs=(hbm, hbm),
        scratch_shapes=[
            tile(ROWS, D),
            tile(ROWS, D),
            tile(D, D),
            tile(D, 2 * D),
            tile(D, D),
            tile(D, FF),
            tile(FF, D),
            tile(16, ROWS, D),
            tile(2, ROWS, D),
            tile(7 * ROWS, 2 * D),
            tile(PAIRS, 2 * ROWS, 128),
            tile(PAIRS, 128, 2 * ROWS),
            tile(PAIRS, 2 * ROWS, 128),
            tile(PAIRS, 128, 2 * ROWS),
            tile(PAIRS, 2 * ROWS, 7 * ROWS, dtype=F32),
            tile(2, PAIRS, 2 * ROWS, 128, dtype=F32),
            tile(2, PAIRS, 2 * ROWS, 128, dtype=F32),
            tile(2, PAIRS, 2 * ROWS, 128, dtype=F32),
            tile(2, PAIRS, 2 * ROWS, 128, dtype=F32),
            tile(ROWS, D),
            tile(PAIRS, 2 * ROWS, 128, dtype=F32),
            tile(2, PAIRS, 2 * ROWS, 128, dtype=F32),
            tile(2 * D, 7 * ROWS),
            tile(5, D, ROWS),
            tile(5, D, ROWS),
            pltpu.SMEM((1, 4), jnp.int32),
            tile(2, D, ROWS),
            tile(2, D, ROWS),
            tile(2, 2, DHALF, ROWS),
            tile(2, D, ROWS),
            tile(2, D, ROWS),
            tile(2, 6, DHALF, ROWS),
            tile(2, DHALF, ROWS),
            tile(2, DHALF, ROWS),
            tile(ROWS, D),
            tile(ROWS, D),
            pltpu.SemaphoreType.DMA((12,)),
            pltpu.SemaphoreType.DMA((25,)),
            pltpu.SemaphoreType.DMA((25,)),
            pltpu.SemaphoreType.DMA((20,)),
            pltpu.SemaphoreType.DMA((20,)),
        ],
        compiler_params=pltpu.CompilerParams(
            collective_id=0, has_side_effects=True, vmem_limit_bytes=60 * 1024 * 1024
        ),
        name="exphormer",
    )(
        experts_list,
        nodes,
        experts_list,
        w_query,
        w_key,
        w_value,
        w_out,
        w_up,
        w_down,
        cotangent,
    )


def solution(mesh):
    return jax.shard_map(
        on_device,
        mesh=mesh,
        in_specs=(
            P(("blk", "dom"), None),
            P(("blk", "dom"), None),
            P(),
            P(),
            P(),
            P(),
            P(),
            P(),
            P(("blk", "dom"), None),
        ),
        out_specs=(P(("blk", "dom"), None), P(("blk", "dom"), None)),
        check_vma=False,
    )
```

time: 366 us -> 61.1 us (0.17)
  the two profiles are of different devices: /device:TPU:8 before, /device:TPU:1 now
where the time goes in v1:
time: 61.1 us; the launch traced here: 60.9 us
  Pallas kernels  58 us (95%)
  local copies, waits for them, and re-layouts  2.26 us (4%)
  between operations  0.65 us (1%)
    pallas_call x1, Pallas kernels, on_device(): pl.pallas_call(kernel, out_shape=(out, out), in_specs=[pl.BlockSpec(memor...  58 us
    unnamed x4, local copies, waits for them, and re-layouts  2.26 us

profile of v1, /device:TPU:1, one launch (start us, length us, event | category | flops | bytes accessed | tf_op | source)
XLA Modules:
  0.0 60.9 jit_solution(7483141702732039719)
XLA Ops:
  0.6 58.0 %exphormer.1 = (bf16[128,512]{1,0:T(8,128)(2,1)}, bf16[128,512]{1,0:T(8,128)(2,1)}) custom-call(s32[1,4]{1,0:T(1,128)} %list_hbm.1, bf16[128,512]{1,0:T(8,128)(2,1)} %nodes_hbm.1, s32[1,4]{1,0:T(1,128)} %list_hbm.1, bf16[512,512]{1,0:T(8,128)(2,1)} %wq_hbm.1, bf16[512,512]{1,0:T(8,128)(2,1)} %wk_hbm.1, bf16[512,512]{1,0:T(8,128)(2,1)} %wv_hbm.1, ...), custom_call_target="tpu_custom_call" | custom-call | tf_op jit(solution)/shard_map/exphormer/pallas_call | solution.py:429
  58.7 0.0 copy-start
  58.7 1.6 %copy.13 = bf16[128,512]{1,0:T(8,128)(2,1)} copy(bf16[128,512]{1,0:T(8,128)(2,1)} %get-tuple-element.4) | data formatting | bytes 262144
  60.3 0.0 copy-done
  60.3 0.7 %copy.14 = bf16[128,512]{1,0:T(8,128)(2,1)} copy(bf16[128,512]{1,0:T(8,128)(2,1)S(1)} %copy-done) | data formatting | bytes 262144
Async XLA Ops:
  58.7 1.6 %copy-start = (bf16[128,512]{1,0:T(8,128)(2,1)S(1)}, bf16[128,512]{1,0:T(8,128)(2,1)}, u32[]{:S(2)}) copy-start(bf16[128,512]{1,0:T(8,128)(2,1)} %get-tuple-element.5) | copy-start | bytes 393220

commit v2 on v1

--- a/solution.py
+++ b/solution.py
@@ -100,8 +100,10 @@
     sbuf,
     tbuf,
     ybuf,
-    outv,
-    goutv,
+    nbuf,
+    actv,
+    residv,
+    gact,
     lsem,
     gsend,
     grecv,
@@ -125,6 +127,10 @@
     up = {"blk": blk, "dom": (dom + 1) % ndom}
     down = {"blk": blk, "dom": (dom + ndom - 1) % ndom}
 
+    barrier = pltpu.get_barrier_semaphore()
+    for peer in (right, left, across, twin, up, down):
+        pl.semaphore_signal(barrier, inc=1, device_id=peer, device_id_type=MESH)
+
     loads = []
 
     def load(src, dst):
@@ -133,18 +139,17 @@
         loads.append(copy)
         return copy
 
+    own = at(x, h, core)
     ld_x = load(nodes_hbm, xv)
     ld_wk = load(wk_hbm, wkv.at[:, pl.ds(0, D)])
     ld_wv = load(wv_hbm, wkv.at[:, pl.ds(D, D)])
     ld_wq = load(wq_hbm, wq)
+    ld_own = load(nodes_hbm, gath.at[own])
+    ld_cot = load(cot_hbm, cotv)
+    ld_wd = load(wd_hbm, wd)
     ld_wo = load(wo_hbm, wo)
     ld_wu = load(wu_hbm, wu)
-    ld_wd = load(wd_hbm, wd)
-    ld_cot = load(cot_hbm, cotv)
-
-    barrier = pltpu.get_barrier_semaphore()
-    for peer in (right, left, across, twin, up, down):
-        pl.semaphore_signal(barrier, inc=1, device_id=peer, device_id_type=MESH)
+
     pl.semaphore_wait(barrier, 6)
 
     sends = []
@@ -164,14 +169,12 @@
 
     top = pl.ds(0, HALF)
     bottom = pl.ds(HALF, HALF)
-    halves = (top, bottom)
 
     def block(xx, rr):
         return at(xx, rr, core)
 
     rows_of = (h, 1 - h)
 
-    own = block(x, h)
     c_r = {}
     c_l = {}
     c_r[0, 0] = push(nodes_hbm.at[top], gath.at[own, top], gsend, grecv, 0, right)
@@ -188,15 +191,13 @@
     c_tw.append(push(nodes_hbm, gath.at[own], gsend, grecv, 16, twin))
 
     ld_x.wait()
-    own_copy = pltpu.make_async_copy(xv, gath.at[own], lsem.at[len(loads)])
-    own_copy.start()
 
     x_full = xv[...].astype(F32)
     unit, inv_std = normalize(x_full)
     normed = unit.astype(BF16)
     ld_wk.wait()
     ld_wv.wait()
-    kv[pl.ds(ROWS, ROWS), :] = dot(normed, wkv[...]).astype(BF16)
+    kv[pl.ds(2 * ROWS, ROWS), :] = dot(normed, wkv[...]).astype(BF16)
     ld_wq.wait()
     queries = dot(normed, wq[...]).astype(BF16) * jnp.asarray(0.125, BF16)
     for hp in range(PAIRS):
@@ -221,6 +222,9 @@
     def to_twin(slot, who):
         c_tw.append(push(gath.at[who], gath.at[who], gsend, grecv, slot, twin))
 
+    ld_wd.wait()
+    ld_cot.wait()
+    gact[...] = dot_t(cotv[...], wd[...])
     forward(0)
     other = block(x, 1 - h)
     c_y[0].wait_recv()
@@ -239,8 +243,8 @@
         unit_o, _ = normalize(raw.astype(F32))
         kv[pl.ds(row0, ROWS), :] = dot(unit_o.astype(BF16), wkv[...]).astype(BF16)
 
-    def attend(base, count, which):
-        for hp in range(PAIRS):
+    def attend(base, count, which, pairs=range(PAIRS)):
+        for hp in pairs:
             k = kv[base : base + count, hp * 128 : (hp + 1) * 128]
             v = kv[base : base + count, D + hp * 128 : D + (hp + 1) * 128]
             s = dot_t(q2[hp], k)
@@ -255,26 +259,29 @@
     c_up.wait_recv()
     project(halo[0], 0)
     c_dn.wait_recv()
-    project(halo[1], 2 * ROWS)
+    project(halo[1], ROWS)
+    attend(0, 3 * ROWS, 0, (0, 1))
+    fwd_r[0].wait_recv()
+    fwd_l[0].wait_recv()
+    to_twin(22, block(x + 2, h))
+    attend(0, 3 * ROWS, 0, (2, 3))
     forward(1)
-    attend(0, 3 * ROWS, 0)
-
-    for rr in (0, 1):
-        if rr == 1:
-            c_r[1, 1].wait_recv()
-            to_twin(20, block(x + 3, 1 - h))
-            c_l[1, 0].wait_recv()
-            to_twin(21, block(x + 1, 1 - h))
-        fwd_r[rr].wait_recv()
-        fwd_l[rr].wait_recv()
-        to_twin(22 + rr, block(x + 2, rows_of[rr]))
+    c_r[1, 1].wait_recv()
+    to_twin(20, block(x + 3, 1 - h))
+    c_l[1, 0].wait_recv()
+    to_twin(21, block(x + 1, 1 - h))
+    fwd_r[1].wait_recv()
+    fwd_l[1].wait_recv()
+    to_twin(23, block(x + 2, 1 - h))
     for copy in c_tw:
         copy.wait_recv()
     c_list.wait_recv()
-    own_copy.wait()
+    ld_own.wait()
 
     for e in range(4):
-        project(gath[listed[0, e]], (3 + e) * ROWS)
+        unit_e, _ = normalize(gath[listed[0, e]].astype(F32))
+        nbuf[e * ROWS : (e + 1) * ROWS] = unit_e.astype(BF16)
+    kv[3 * ROWS : 7 * ROWS, :] = dot(nbuf[...], wkv[...]).astype(BF16)
     attend(3 * ROWS, 4 * ROWS, 1)
 
     for hp in range(PAIRS):
@@ -294,19 +301,15 @@
     unit2, inv_std2 = normalize(resid)
     ld_wu.wait()
     pre = dot(unit2.astype(BF16), wu[...])
-    ld_wd.wait()
-    ld_cot.wait()
     cot = cotv[...]
-    grad_act = dot_t(cot, wd[...])
     c0 = 0.7978845608028654
     sq = pre * pre
     th = jnp.tanh(c0 * (pre + 0.044715 * (sq * pre)))
     act = 0.5 * pre * (1.0 + th)
     slope = 0.5 * (1.0 + th) + 0.5 * pre * (1.0 - th * th) * (c0 * (1.0 + 3.0 * 0.044715 * sq))
-    outv[...] = (resid + dot(act.astype(BF16), wd[...])).astype(BF16)
-    st_out = pltpu.make_async_copy(outv, out_hbm, lsem.at[len(loads) + 1])
-    st_out.start()
-    grad_pre = (grad_act * slope).astype(BF16)
+    actv[...] = act.astype(BF16)
+    residv[...] = resid
+    grad_pre = (gact[...] * slope).astype(BF16)
     grad_norm2 = dot_t(grad_pre, wu[...])
     grad_resid = cot.astype(F32) + normalize_back(unit2, inv_std2, grad_norm2)
     grad_mixed = dot_t(grad_resid.astype(BF16), wo[...]).astype(BF16)
@@ -319,8 +322,8 @@
         d = jnp.sum(stacked.astype(F32) * both, axis=1, keepdims=True)
         delt[hp] = jnp.broadcast_to(d, (2 * ROWS, 128))
 
-    def attend_back(base, count, which):
-        for hp in range(PAIRS):
+    def attend_back(base, count, which, pairs=range(PAIRS)):
+        for hp in pairs:
             k = kv[base : base + count, hp * 128 : (hp + 1) * 128]
             v = kv[base : base + count, D + hp * 128 : D + (hp + 1) * 128]
             p = wexp[hp, :, base : base + count] * fstat[which, hp][:, :1]
@@ -330,8 +333,7 @@
             dt[D + hp * 128 : D + (hp + 1) * 128, base : base + count] = dot(
                 g2t[hp], p.astype(BF16)
             ).astype(BF16)
-            dq_part = dot(ds, k)
-            dq[which, hp] = dq_part
+            dq[which, hp] = dot(ds, k)
 
     attend_back(3 * ROWS, 4 * ROWS, 1)
 
@@ -339,17 +341,14 @@
     part[4] = zero_block
     psib[4] = zero_block
     c_ps = []
-    for e in range(4):
-        cols = slice((3 + e) * ROWS, (4 + e) * ROWS)
-        part[e] = dot(wkv[...], dt[:, cols]).astype(BF16)
+    for e in (0, 2):
+        both = dot(wkv[...], dt[:, (3 + e) * ROWS : (5 + e) * ROWS]).astype(BF16)
+        part[e] = both[:, :ROWS]
+        part[e + 1] = both[:, ROWS:]
         c_ps.append(push(part.at[e], psib.at[e], rsend, rrecv, e, twin))
-
-    attend_back(0, 3 * ROWS, 0)
-    hsend[0] = dot(wkv[...], dt[:, 0:ROWS]).astype(BF16)
-    c_hd = push(hsend.at[0], hrecv.at[0], rsend, rrecv, 4, down)
-    hsend[1] = dot(wkv[...], dt[:, 2 * ROWS : 3 * ROWS]).astype(BF16)
-    c_hu = push(hsend.at[1], hrecv.at[1], rsend, rrecv, 5, up)
-
+        c_ps.append(push(part.at[e + 1], psib.at[e + 1], rsend, rrecv, e + 1, twin))
+
+    attend_back(0, 3 * ROWS, 0, (0, 1, 2))
     for copy in c_ps:
         copy.wait_recv()
 
@@ -370,7 +369,8 @@
     db = pl.ds(DHALF, DHALF)
 
     c_x = {}
-    for rr in (1, 0):
+
+    def first_step(rr):
         s0 = 8 + 6 * rr
         sbuf[rr, 0] = summed(x + 2, rr, da).astype(BF16)
         c_x[rr, 0] = push(sbuf.at[rr, 0], xo.at[rr, 0], rsend, rrecv, s0, right)
@@ -380,7 +380,8 @@
         c_x[rr, 2] = push(sbuf.at[rr, 2], yl.at[rr, db], rsend, rrecv, s0 + 2, right)
         sbuf[rr, 3] = summed(x + 3, rr, da).astype(BF16)
         c_x[rr, 3] = push(sbuf.at[rr, 3], yr.at[rr, da], rsend, rrecv, s0 + 3, left)
-    for rr in (1, 0):
+
+    def second_step(rr):
         s0 = 8 + 6 * rr
         c_x[rr, 0].wait_recv()
         sbuf[rr, 4] = (summed(x + 1, rr, da) + xo[rr, 0].astype(F32)).astype(BF16)
@@ -389,10 +390,22 @@
         sbuf[rr, 5] = (summed(x + 3, rr, db) + xo[rr, 1].astype(F32)).astype(BF16)
         c_x[rr, 5] = push(sbuf.at[rr, 5], yr.at[rr, db], rsend, rrecv, s0 + 5, left)
 
-    own_t = dot(wkv[...], dt[:, ROWS : 2 * ROWS])
+    first_step(1)
+    attend_back(0, 3 * ROWS, 0, (3,))
+    halves_t = dot(wkv[...], dt[:, 0 : 2 * ROWS]).astype(BF16)
+    hsend[0] = halves_t[:, :ROWS]
+    hsend[1] = halves_t[:, ROWS:]
+    c_hd = push(hsend.at[0], hrecv.at[0], rsend, rrecv, 4, down)
+    c_hu = push(hsend.at[1], hrecv.at[1], rsend, rrecv, 5, up)
+    second_step(1)
+    first_step(0)
+
+    own_t = dot(wkv[...], dt[:, 2 * ROWS : 3 * ROWS])
     grad_q = jnp.concatenate([head_join(dq[0, hp] + dq[1, hp]) for hp in range(PAIRS)], 1)
     grad_in = dot_t((grad_q * 0.125).astype(BF16), wq[...])
-
+    out_hbm[...] = (residv[...] + dot(actv[...], wd[...])).astype(BF16)
+
+    second_step(0)
     for slot in (2, 3, 4, 5):
         c_x[1, slot].wait_recv()
     for i, cols in enumerate((da, db)):
@@ -407,30 +420,27 @@
         c_x[0, slot].wait_recv()
     own_t = own_t + yl[0].astype(F32) + yr[0].astype(F32)
     own_t = own_t + jnp.concatenate([summed(x, 0, da), summed(x, 0, db)], 0)
+    grad_in = grad_in + jnp.transpose(own_t)
+    unit_b, inv_b = normalize(xv[...].astype(F32))
     c_x[2, 0].wait_recv()
     c_x[2, 1].wait_recv()
-    own_t = own_t + jnp.concatenate([ybuf[0], ybuf[1]], 0).astype(F32)
-    grad_in = grad_in + jnp.transpose(own_t)
-    unit_b, inv_b = normalize(xv[...].astype(F32))
-    goutv[...] = (grad_resid + normalize_back(unit_b, inv_b, grad_in)).astype(BF16)
-    st_gout = pltpu.make_async_copy(goutv, gout_hbm, lsem.at[len(loads) + 2])
-    st_gout.start()
+    grad_in = grad_in + jnp.transpose(jnp.concatenate([ybuf[0], ybuf[1]], 0).astype(F32))
+    gout_hbm[...] = (grad_resid + normalize_back(unit_b, inv_b, grad_in)).astype(BF16)
     for copy in sends:
         copy.wait_send()
-    st_out.wait()
-    st_gout.wait()
 
 
 def on_device(nodes, experts_list, w_query, w_key, w_value, w_out, w_up, w_down, cotangent):
     rows, width = nodes.shape
-    hbm = pl.BlockSpec(memory_space=pl.ANY)
+    hbm = pl.BlockSpec(memory_space=pltpu.HBM)
     tile = lambda *shape, dtype=BF16: pltpu.VMEM(shape, dtype)
     out = jax.ShapeDtypeStruct((rows, width), BF16)
+    vm = pl.BlockSpec(memory_space=pltpu.VMEM)
     return pl.pallas_call(
         kernel,
         out_shape=(out, out),
         in_specs=[pl.BlockSpec(memory_space=pltpu.SMEM)] + [hbm] * 9,
-        out_specs=(hbm, hbm),
+        out_specs=(vm, vm),
         scratch_shapes=[
             tile(ROWS, D),
             tile(ROWS, D),
@@ -466,8 +476,10 @@
             tile(2, 6, DHALF, ROWS),
             tile(2, DHALF, ROWS),
             tile(2, DHALF, ROWS),
-            tile(ROWS, D),
-            tile(ROWS, D),
+            tile(4 * ROWS, D),
+            tile(ROWS, FF),
+            tile(ROWS, D, dtype=F32),
+            tile(ROWS, FF, dtype=F32),
             pltpu.SemaphoreType.DMA((12,)),
             pltpu.SemaphoreType.DMA((25,)),
             pltpu.SemaphoreType.DMA((25,)),
@@ -475,20 +487,15 @@
             pltpu.SemaphoreType.DMA((20,)),
         ],
         compiler_params=pltpu.CompilerParams(
-            collective_id=0, has_side_effects=True, vmem_limit_bytes=60 * 1024 * 1024
+            collective_id=0, has_side_effects=True, vmem_limit_bytes=28 * 1024 * 1024
         ),
         name="exphormer",
     )(
         experts_list,
-        nodes,
-        experts_list,
-        w_query,
-        w_key,
-        w_value,
-        w_out,
-        w_up,
-        w_down,
-        cotangent,
+        *(
+            pltpu.with_memory_space_constraint(a, pltpu.HBM)
+            for a in (nodes, experts_list, w_query, w_key, w_value, w_out, w_up, w_down, cotangent)
+        ),
     )
 
 

time: 61.1 us -> 54.3 us (0.89)
  the two profiles are of different devices: /device:TPU:1 before, /device:TPU:2 now
where the time goes in v2:
time: 54.3 us; the launch traced here: 54.1 us
  Pallas kernels  52.2 us (96%)
  local copies, waits for them, and re-layouts  1.31 us (2%)
  between operations  0.64 us (1%)
    pallas_call x1, Pallas kernels, on_device(): pl.pallas_call(kernel, out_shape=(out, out), in_specs=[pl.BlockSpec(memor...  52.2 us
    unnamed x2, local copies, waits for them, and re-layouts  1.31 us

profile of v2, /device:TPU:2, one launch (start us, length us, event | category | flops | bytes accessed | tf_op | source)
XLA Modules:
  0.0 54.1 jit_solution(7935244711296825659)
XLA Ops:
  0.6 52.2 %exphormer.1 = (bf16[128,512]{1,0:T(8,128)(2,1)S(1)}, bf16[128,512]{1,0:T(8,128)(2,1)S(1)}) custom-call(s32[1,4]{1,0:T(1,128)} %list_hbm.1, bf16[128,512]{1,0:T(8,128)(2,1)} %nodes_hbm.1, s32[1,4]{1,0:T(1,128)} %list_hbm.1, bf16[512,512]{1,0:T(8,128)(2,1)} %wq_hbm.1, bf16[512,512]{1,0:T(8,128)(2,1)} %wk_hbm.1, bf16[512,512]{1,0:T(8,128)(2,1)} %wv_hbm.1, ...), custom_call_target="tpu_custom_call" | custom-call | tf_op jit(solution)/shard_map/exphormer/pallas_call | solution.py:439
  52.8 0.7 %copy.13 = bf16[128,512]{1,0:T(8,128)(2,1)} copy(bf16[128,512]{1,0:T(8,128)(2,1)S(1)} %get-tuple-element.4) | data formatting | bytes 262144
  53.5 0.7 %copy.14 = bf16[128,512]{1,0:T(8,128)(2,1)} copy(bf16[128,512]{1,0:T(8,128)(2,1)S(1)} %get-tuple-element.5) | data formatting | bytes 262144

commit v3 on v2

--- a/solution.py
+++ b/solution.py
@@ -131,25 +131,6 @@
     for peer in (right, left, across, twin, up, down):
         pl.semaphore_signal(barrier, inc=1, device_id=peer, device_id_type=MESH)
 
-    loads = []
-
-    def load(src, dst):
-        copy = pltpu.make_async_copy(src, dst, lsem.at[len(loads)])
-        copy.start()
-        loads.append(copy)
-        return copy
-
-    own = at(x, h, core)
-    ld_x = load(nodes_hbm, xv)
-    ld_wk = load(wk_hbm, wkv.at[:, pl.ds(0, D)])
-    ld_wv = load(wv_hbm, wkv.at[:, pl.ds(D, D)])
-    ld_wq = load(wq_hbm, wq)
-    ld_own = load(nodes_hbm, gath.at[own])
-    ld_cot = load(cot_hbm, cotv)
-    ld_wd = load(wd_hbm, wd)
-    ld_wo = load(wo_hbm, wo)
-    ld_wu = load(wu_hbm, wu)
-
     pl.semaphore_wait(barrier, 6)
 
     sends = []
@@ -175,23 +156,39 @@
 
     rows_of = (h, 1 - h)
 
+    own = block(x, h)
     c_r = {}
     c_l = {}
+    c_y = []
+    c_y.append(push(nodes_hbm.at[top], gath.at[own, top], gsend, grecv, 12, across))
     c_r[0, 0] = push(nodes_hbm.at[top], gath.at[own, top], gsend, grecv, 0, right)
     c_l[0, 1] = push(nodes_hbm.at[bottom], gath.at[own, bottom], gsend, grecv, 5, left)
-    c_y = [None, None]
-    c_y[0] = push(nodes_hbm.at[top], gath.at[own, top], gsend, grecv, 12, across)
-    c_y[1] = push(nodes_hbm.at[bottom], gath.at[own, bottom], gsend, grecv, 13, across)
+    c_y.append(push(nodes_hbm.at[bottom], gath.at[own, bottom], gsend, grecv, 13, across))
     c_r[0, 1] = push(nodes_hbm.at[bottom], gath.at[own, bottom], gsend, grecv, 1, right)
     c_l[0, 0] = push(nodes_hbm.at[top], gath.at[own, top], gsend, grecv, 4, left)
-    c_up = push(nodes_hbm, halo.at[0], gsend, grecv, 14, up)
-    c_dn = push(nodes_hbm, halo.at[1], gsend, grecv, 15, down)
+
+    loads = []
+
+    def load(src, dst):
+        copy = pltpu.make_async_copy(src, dst, lsem.at[len(loads)])
+        copy.start()
+        loads.append(copy)
+        return copy
+
+    ld_x = load(nodes_hbm, xv)
+    ld_wk = load(wk_hbm, wkv.at[:, pl.ds(0, D)])
+    ld_wv = load(wv_hbm, wkv.at[:, pl.ds(D, D)])
+    ld_wq = load(wq_hbm, wq)
+    ld_own = load(nodes_hbm, gath.at[own])
+    ld_cot = load(cot_hbm, cotv)
+    ld_wd = load(wd_hbm, wd)
+    ld_wo = load(wo_hbm, wo)
+    ld_wu = load(wu_hbm, wu)
+
     c_list = push(list_hbm, lsib, gsend, grecv, 24, twin)
-    c_tw = []
-    c_tw.append(push(nodes_hbm, gath.at[own], gsend, grecv, 16, twin))
+    c_tw = [push(nodes_hbm, gath.at[own], gsend, grecv, 16, twin)]
 
     ld_x.wait()
-
     x_full = xv[...].astype(F32)
     unit, inv_std = normalize(x_full)
     normed = unit.astype(BF16)
@@ -222,6 +219,8 @@
     def to_twin(slot, who):
         c_tw.append(push(gath.at[who], gath.at[who], gsend, grecv, slot, twin))
 
+    c_up = push(nodes_hbm, halo.at[0], gsend, grecv, 14, up)
+    c_dn = push(nodes_hbm, halo.at[1], gsend, grecv, 15, down)
     ld_wd.wait()
     ld_cot.wait()
     gact[...] = dot_t(cotv[...], wd[...])
@@ -256,20 +255,19 @@
             mstat[which, hp] = jnp.broadcast_to(m, (2 * ROWS, 128))
             lstat[which, hp] = jnp.broadcast_to(total, (2 * ROWS, 128))
 
+    forward(1)
+    fwd_r[0].wait_recv()
+    fwd_l[0].wait_recv()
+    to_twin(22, block(x + 2, h))
     c_up.wait_recv()
     project(halo[0], 0)
     c_dn.wait_recv()
     project(halo[1], ROWS)
-    attend(0, 3 * ROWS, 0, (0, 1))
-    fwd_r[0].wait_recv()
-    fwd_l[0].wait_recv()
-    to_twin(22, block(x + 2, h))
-    attend(0, 3 * ROWS, 0, (2, 3))
-    forward(1)
     c_r[1, 1].wait_recv()
     to_twin(20, block(x + 3, 1 - h))
     c_l[1, 0].wait_recv()
     to_twin(21, block(x + 1, 1 - h))
+    attend(0, 3 * ROWS, 0)
     fwd_r[1].wait_recv()
     fwd_l[1].wait_recv()
     to_twin(23, block(x + 2, 1 - h))
@@ -370,12 +368,15 @@
 
     c_x = {}
 
-    def first_step(rr):
+    def opposite_step(rr):
         s0 = 8 + 6 * rr
         sbuf[rr, 0] = summed(x + 2, rr, da).astype(BF16)
         c_x[rr, 0] = push(sbuf.at[rr, 0], xo.at[rr, 0], rsend, rrecv, s0, right)
         sbuf[rr, 1] = summed(x + 2, rr, db).astype(BF16)
         c_x[rr, 1] = push(sbuf.at[rr, 1], xo.at[rr, 1], rsend, rrecv, s0 + 1, left)
+
+    def direct_step(rr):
+        s0 = 8 + 6 * rr
         sbuf[rr, 2] = summed(x + 1, rr, db).astype(BF16)
         c_x[rr, 2] = push(sbuf.at[rr, 2], yl.at[rr, db], rsend, rrecv, s0 + 2, right)
         sbuf[rr, 3] = summed(x + 3, rr, da).astype(BF16)
@@ -390,22 +391,23 @@
         sbuf[rr, 5] = (summed(x + 3, rr, db) + xo[rr, 1].astype(F32)).astype(BF16)
         c_x[rr, 5] = push(sbuf.at[rr, 5], yr.at[rr, db], rsend, rrecv, s0 + 5, left)
 
-    first_step(1)
+    opposite_step(1)
     attend_back(0, 3 * ROWS, 0, (3,))
     halves_t = dot(wkv[...], dt[:, 0 : 2 * ROWS]).astype(BF16)
     hsend[0] = halves_t[:, :ROWS]
     hsend[1] = halves_t[:, ROWS:]
     c_hd = push(hsend.at[0], hrecv.at[0], rsend, rrecv, 4, down)
     c_hu = push(hsend.at[1], hrecv.at[1], rsend, rrecv, 5, up)
+    direct_step(1)
     second_step(1)
-    first_step(0)
+    opposite_step(0)
+    direct_step(0)
 
     own_t = dot(wkv[...], dt[:, 2 * ROWS : 3 * ROWS])
     grad_q = jnp.concatenate([head_join(dq[0, hp] + dq[1, hp]) for hp in range(PAIRS)], 1)
     grad_in = dot_t((grad_q * 0.125).astype(BF16), wq[...])
     out_hbm[...] = (residv[...] + dot(actv[...], wd[...])).astype(BF16)
 
-    second_step(0)
     for slot in (2, 3, 4, 5):
         c_x[1, slot].wait_recv()
     for i, cols in enumerate((da, db)):
@@ -413,6 +415,7 @@
             summed(x, 1, cols) + yl[1, cols, :].astype(F32) + yr[1, cols, :].astype(F32)
         ).astype(BF16)
         c_x[2, i] = push(tbuf.at[i], ybuf.at[i], rsend, rrecv, 6 + i, across)
+    second_step(0)
     c_hd.wait_recv()
     c_hu.wait_recv()
     own_t = own_t + hrecv[0].astype(F32) + hrecv[1].astype(F32)

time: 54.3 us -> 54.1 us (level)
  the two profiles are of different devices: /device:TPU:2 before, /device:TPU:4 now
where the time goes in v3:
time: 54.1 us; the launch traced here: 54 us
  Pallas kernels  52.1 us (96%)
  local copies, waits for them, and re-layouts  1.31 us (2%)
  between operations  0.64 us (1%)
    pallas_call x1, Pallas kernels, on_device(): pl.pallas_call(kernel, out_shape=(out, out), in_specs=[pl.BlockSpec(memor...  52.1 us
    unnamed x2, local copies, waits for them, and re-layouts  1.31 us

profile of v3, /device:TPU:4, one launch (start us, length us, event | category | flops | bytes accessed | tf_op | source)
XLA Modules:
  0.0 54.0 jit_solution(5705210810672929266)
XLA Ops:
  0.6 52.1 %exphormer.1 = (bf16[128,512]{1,0:T(8,128)(2,1)S(1)}, bf16[128,512]{1,0:T(8,128)(2,1)S(1)}) custom-call(s32[1,4]{1,0:T(1,128)} %list_hbm.1, bf16[128,512]{1,0:T(8,128)(2,1)} %nodes_hbm.1, s32[1,4]{1,0:T(1,128)} %list_hbm.1, bf16[512,512]{1,0:T(8,128)(2,1)} %wq_hbm.1, bf16[512,512]{1,0:T(8,128)(2,1)} %wk_hbm.1, bf16[512,512]{1,0:T(8,128)(2,1)} %wv_hbm.1, ...), custom_call_target="tpu_custom_call" | custom-call | tf_op jit(solution)/shard_map/exphormer/pallas_call | solution.py:442
  52.7 0.7 %copy.13 = bf16[128,512]{1,0:T(8,128)(2,1)} copy(bf16[128,512]{1,0:T(8,128)(2,1)S(1)} %get-tuple-element.4) | data formatting | bytes 262144
  53.4 0.7 %copy.14 = bf16[128,512]{1,0:T(8,128)(2,1)} copy(bf16[128,512]{1,0:T(8,128)(2,1)S(1)} %get-tuple-element.5) | data formatting | bytes 262144

commit v4 on v3

--- a/solution.py
+++ b/solution.py
@@ -105,6 +105,7 @@
     residv,
     gact,
     lsem,
+    ready,
     gsend,
     grecv,
     rsend,
@@ -127,15 +128,39 @@
     up = {"blk": blk, "dom": (dom + 1) % ndom}
     down = {"blk": blk, "dom": (dom + ndom - 1) % ndom}
 
+    half = ndom // 2
+    z = dom % half
+    final = half - 1
+
     barrier = pltpu.get_barrier_semaphore()
-    for peer in (right, left, across, twin, up, down):
+
+    def greet(peer):
         pl.semaphore_signal(barrier, inc=1, device_id=peer, device_id_type=MESH)
 
-    pl.semaphore_wait(barrier, 6)
+    for peer in (right, left, across, twin):
+        greet(peer)
+
+    @pl.when(z < final)
+    def _():
+        greet(up)
+
+    @pl.when(z == 0)
+    def _():
+        greet(down)
+
+    pl.semaphore_wait(barrier, 4 + jnp.where(z > 0, 1, 0) + jnp.where(z == final, 1, 0))
+
+    @pl.when(z > 0)
+    def _():
+        pl.semaphore_signal(ready.at[0], inc=1, device_id=down, device_id_type=MESH)
+
+    @pl.when(z == final)
+    def _():
+        pl.semaphore_signal(ready.at[1], inc=1, device_id=up, device_id_type=MESH)
 
     sends = []
 
-    def push(src, dst, ssems, rsems, slot, peer):
+    def plan(src, dst, ssems, rsems, slot, peer):
         copy = pltpu.make_async_remote_copy(
             src_ref=src,
             dst_ref=dst,
@@ -144,8 +169,12 @@
             device_id=peer,
             device_id_type=MESH,
         )
+        sends.append(copy)
+        return copy
+
+    def push(*where):
+        copy = plan(*where)
         copy.start()
-        sends.append(copy)
         return copy
 
     top = pl.ds(0, HALF)
@@ -219,8 +248,17 @@
     def to_twin(slot, who):
         c_tw.append(push(gath.at[who], gath.at[who], gsend, grecv, slot, twin))
 
-    c_up = push(nodes_hbm, halo.at[0], gsend, grecv, 14, up)
-    c_dn = push(nodes_hbm, halo.at[1], gsend, grecv, 15, down)
+    c_up = plan(nodes_hbm, halo.at[0], gsend, grecv, 14, up)
+    c_dn = plan(nodes_hbm, halo.at[1], gsend, grecv, 15, down)
+
+    @pl.when(z > 0)
+    def _():
+        c_dn.start()
+
+    @pl.when(z == final)
+    def _():
+        c_up.start()
+
     ld_wd.wait()
     ld_cot.wait()
     gact[...] = dot_t(cotv[...], wd[...])
@@ -238,6 +276,12 @@
     c_l[0, 0].wait_recv()
     to_twin(19, block(x + 1, h))
 
+    @pl.when(z < final)
+    def _():
+        pl.semaphore_wait(ready.at[0], 1)
+        c_up.start()
+
+
     def project(raw, row0):
         unit_o, _ = normalize(raw.astype(F32))
         kv[pl.ds(row0, ROWS), :] = dot(unit_o.astype(BF16), wkv[...]).astype(BF16)
@@ -259,6 +303,11 @@
     fwd_r[0].wait_recv()
     fwd_l[0].wait_recv()
     to_twin(22, block(x + 2, h))
+    @pl.when(z == 0)
+    def _():
+        pl.semaphore_wait(ready.at[1], 1)
+        c_dn.start()
+
     c_up.wait_recv()
     project(halo[0], 0)
     c_dn.wait_recv()
@@ -483,7 +532,8 @@
             tile(ROWS, FF),
             tile(ROWS, D, dtype=F32),
             tile(ROWS, FF, dtype=F32),
-            pltpu.SemaphoreType.DMA((12,)),
+            pltpu.SemaphoreType.DMA((9,)),
+            pltpu.SemaphoreType.REGULAR((2,)),
             pltpu.SemaphoreType.DMA((25,)),
             pltpu.SemaphoreType.DMA((25,)),
             pltpu.SemaphoreType.DMA((20,)),

time: 54.1 us -> 49.1 us (0.908)
  the two profiles are of different devices: /device:TPU:4 before, /device:TPU:2 now
where the time goes in v4:
time: 49.1 us; the launch traced here: 48.9 us
  Pallas kernels  47 us (96%)
  local copies, waits for them, and re-layouts  1.31 us (3%)
  between operations  0.64 us (1%)
    pallas_call x1, Pallas kernels, on_device(): pl.pallas_call(kernel, out_shape=(out, out), in_specs=[pl.BlockSpec(memor...  47 us
    unnamed x2, local copies, waits for them, and re-layouts  1.31 us

profile of v4, /device:TPU:2, one launch (start us, length us, event | category | flops | bytes accessed | tf_op | source)
XLA Modules:
  0.0 48.9 jit_solution(849914512335906347)
XLA Ops:
  0.6 47.0 %exphormer.1 = (bf16[128,512]{1,0:T(8,128)(2,1)S(1)}, bf16[128,512]{1,0:T(8,128)(2,1)S(1)}) custom-call(s32[1,4]{1,0:T(1,128)} %list_hbm.1, bf16[128,512]{1,0:T(8,128)(2,1)} %nodes_hbm.1, s32[1,4]{1,0:T(1,128)} %list_hbm.1, bf16[512,512]{1,0:T(8,128)(2,1)} %wq_hbm.1, bf16[512,512]{1,0:T(8,128)(2,1)} %wk_hbm.1, bf16[512,512]{1,0:T(8,128)(2,1)} %wv_hbm.1, ...), custom_call_target="tpu_custom_call" | custom-call | tf_op jit(solution)/shard_map/exphormer/pallas_call | solution.py:491
  47.6 0.7 %copy.13 = bf16[128,512]{1,0:T(8,128)(2,1)} copy(bf16[128,512]{1,0:T(8,128)(2,1)S(1)} %get-tuple-element.4) | data formatting | bytes 262144
  48.3 0.7 %copy.14 = bf16[128,512]{1,0:T(8,128)(2,1)} copy(bf16[128,512]{1,0:T(8,128)(2,1)S(1)} %get-tuple-element.5) | data formatting | bytes 262144

commit v5 on v4

--- a/solution.py
+++ b/solution.py
@@ -80,6 +80,9 @@
     q2t,
     g2,
     g2t,
+    dpv,
+    pbv,
+    dsv,
     wexp,
     mstat,
     lstat,
@@ -106,9 +109,8 @@
     gact,
     lsem,
     ready,
-    gsend,
+    ssem,
     grecv,
-    rsend,
     rrecv,
 ):
     blk = lax.axis_index("blk")
@@ -160,17 +162,28 @@
 
     sends = []
 
-    def plan(src, dst, ssems, rsems, slot, peer):
+    pool = list(range(19))
+
+    def plan(src, dst, rsems, slot, peer):
+        index = pool.pop(0)
         copy = pltpu.make_async_remote_copy(
             src_ref=src,
             dst_ref=dst,
-            send_sem=ssems.at[slot],
+            send_sem=ssem.at[index],
             recv_sem=rsems.at[slot],
             device_id=peer,
             device_id_type=MESH,
         )
-        sends.append(copy)
+        sends.append((copy, index))
         return copy
+
+    def reclaim(keep=()):
+        held = [entry for entry in sends if any(entry[0] is copy for copy in keep)]
+        for copy, index in sends:
+            if not any(copy is entry[0] for entry in held):
+                copy.wait_send()
+                pool.append(index)
+        sends[:] = held
 
     def push(*where):
         copy = plan(*where)
@@ -189,12 +202,12 @@
     c_r = {}
     c_l = {}
     c_y = []
-    c_y.append(push(nodes_hbm.at[top], gath.at[own, top], gsend, grecv, 12, across))
-    c_r[0, 0] = push(nodes_hbm.at[top], gath.at[own, top], gsend, grecv, 0, right)
-    c_l[0, 1] = push(nodes_hbm.at[bottom], gath.at[own, bottom], gsend, grecv, 5, left)
-    c_y.append(push(nodes_hbm.at[bottom], gath.at[own, bottom], gsend, grecv, 13, across))
-    c_r[0, 1] = push(nodes_hbm.at[bottom], gath.at[own, bottom], gsend, grecv, 1, right)
-    c_l[0, 0] = push(nodes_hbm.at[top], gath.at[own, top], gsend, grecv, 4, left)
+    c_y.append(push(nodes_hbm.at[top], gath.at[own, top], grecv, 12, across))
+    c_r[0, 0] = push(nodes_hbm.at[top], gath.at[own, top], grecv, 0, right)
+    c_l[0, 1] = push(nodes_hbm.at[bottom], gath.at[own, bottom], grecv, 5, left)
+    c_y.append(push(nodes_hbm.at[bottom], gath.at[own, bottom], grecv, 13, across))
+    c_r[0, 1] = push(nodes_hbm.at[bottom], gath.at[own, bottom], grecv, 1, right)
+    c_l[0, 0] = push(nodes_hbm.at[top], gath.at[own, top], grecv, 4, left)
 
     loads = []
 
@@ -214,8 +227,8 @@
     ld_wo = load(wo_hbm, wo)
     ld_wu = load(wu_hbm, wu)
 
-    c_list = push(list_hbm, lsib, gsend, grecv, 24, twin)
-    c_tw = [push(nodes_hbm, gath.at[own], gsend, grecv, 16, twin)]
+    c_list = push(list_hbm, lsib, grecv, 24, twin)
+    c_tw = [push(nodes_hbm, gath.at[own], grecv, 16, twin)]
 
     ld_x.wait()
     x_full = xv[...].astype(F32)
@@ -238,18 +251,18 @@
         row = rows_of[rr]
         c_r[rr, 0].wait_recv()
         from_left = block(x + 3, row)
-        fwd_r[rr] = push(gath.at[from_left, top], gath.at[from_left, top], gsend, grecv, 8 + rr, right)
+        fwd_r[rr] = push(gath.at[from_left, top], gath.at[from_left, top], grecv, 8 + rr, right)
         c_l[rr, 1].wait_recv()
         from_right = block(x + 1, row)
         fwd_l[rr] = push(
-            gath.at[from_right, bottom], gath.at[from_right, bottom], gsend, grecv, 10 + rr, left
+            gath.at[from_right, bottom], gath.at[from_right, bottom], grecv, 10 + rr, left
         )
 
     def to_twin(slot, who):
-        c_tw.append(push(gath.at[who], gath.at[who], gsend, grecv, slot, twin))
-
-    c_up = plan(nodes_hbm, halo.at[0], gsend, grecv, 14, up)
-    c_dn = plan(nodes_hbm, halo.at[1], gsend, grecv, 15, down)
+        c_tw.append(push(gath.at[who], gath.at[who], grecv, slot, twin))
+
+    c_up = plan(nodes_hbm, halo.at[0], grecv, 14, up)
+    c_dn = plan(nodes_hbm, halo.at[1], grecv, 15, down)
 
     @pl.when(z > 0)
     def _():
@@ -265,11 +278,11 @@
     forward(0)
     other = block(x, 1 - h)
     c_y[0].wait_recv()
-    c_r[1, 0] = push(gath.at[other, top], gath.at[other, top], gsend, grecv, 2, right)
-    c_l[1, 0] = push(gath.at[other, top], gath.at[other, top], gsend, grecv, 6, left)
+    c_r[1, 0] = push(gath.at[other, top], gath.at[other, top], grecv, 2, right)
+    c_l[1, 0] = push(gath.at[other, top], gath.at[other, top], grecv, 6, left)
     c_y[1].wait_recv()
-    c_l[1, 1] = push(gath.at[other, bottom], gath.at[other, bottom], gsend, grecv, 7, left)
-    c_r[1, 1] = push(gath.at[other, bottom], gath.at[other, bottom], gsend, grecv, 3, right)
+    c_l[1, 1] = push(gath.at[other, bottom], gath.at[other, bottom], grecv, 7, left)
+    c_r[1, 1] = push(gath.at[other, bottom], gath.at[other, bottom], grecv, 3, right)
     to_twin(17, other)
     c_r[0, 1].wait_recv()
     to_twin(18, block(x + 3, h))
@@ -289,16 +302,20 @@
     def attend(base, count, which, pairs=range(PAIRS)):
         for hp in pairs:
             k = kv[base : base + count, hp * 128 : (hp + 1) * 128]
-            v = kv[base : base + count, D + hp * 128 : D + (hp + 1) * 128]
-            s = dot_t(q2[hp], k)
+            wexp[hp, :, base : base + count] = dot_t(q2[hp], k)
+        for hp in pairs:
+            s = wexp[hp, :, base : base + count]
             m = jnp.max(s, axis=1, keepdims=True)
             w = jnp.exp(s - m)
             wexp[hp, :, base : base + count] = w
             total = jnp.sum(w, axis=1, keepdims=True)
-            oacc[which, hp] = dot(w.astype(BF16), v)
             mstat[which, hp] = jnp.broadcast_to(m, (2 * ROWS, 128))
             lstat[which, hp] = jnp.broadcast_to(total, (2 * ROWS, 128))
-
+        for hp in pairs:
+            v = kv[base : base + count, D + hp * 128 : D + (hp + 1) * 128]
+            oacc[which, hp] = dot(wexp[hp, :, base : base + count].astype(BF16), v)
+
+    reclaim([copy for copy, _ in sends[8:]])
     forward(1)
     fwd_r[0].wait_recv()
     fwd_l[0].wait_recv()
@@ -369,33 +386,46 @@
         d = jnp.sum(stacked.astype(F32) * both, axis=1, keepdims=True)
         delt[hp] = jnp.broadcast_to(d, (2 * ROWS, 128))
 
-    def attend_back(base, count, which, pairs=range(PAIRS)):
-        for hp in pairs:
+    def attend_back(base, count, which):
+        tiles = count // 128
+        for hp in range(PAIRS):
+            v = kv[base : base + count, D + hp * 128 : D + (hp + 1) * 128]
+            dpv[hp, :, :count] = dot_t(g2[hp], v)
+        for hp in range(PAIRS):
+            scale = jnp.concatenate([fstat[which, hp]] * tiles, 1)
+            shift = jnp.concatenate([delt[hp]] * tiles, 1)
+            p = wexp[hp, :, base : base + count] * scale
+            pbv[hp, :, :count] = p.astype(BF16)
+            dsv[hp, :, :count] = (p * (dpv[hp, :, :count] - shift)).astype(BF16)
+        for hp in range(PAIRS):
+            dt[D + hp * 128 : D + (hp + 1) * 128, base : base + count] = dot(
+                g2t[hp], pbv[hp, :, :count]
+            ).astype(BF16)
+            dt[hp * 128 : (hp + 1) * 128, base : base + count] = dot(
+                q2t[hp], dsv[hp, :, :count]
+            ).astype(BF16)
             k = kv[base : base + count, hp * 128 : (hp + 1) * 128]
-            v = kv[base : base + count, D + hp * 128 : D + (hp + 1) * 128]
-            p = wexp[hp, :, base : base + count] * fstat[which, hp][:, :1]
-            dp = dot_t(g2[hp], v)
-            ds = (p * (dp - delt[hp][:, :1])).astype(BF16)
-            dt[hp * 128 : (hp + 1) * 128, base : base + count] = dot(q2t[hp], ds).astype(BF16)
-            dt[D + hp * 128 : D + (hp + 1) * 128, base : base + count] = dot(
-                g2t[hp], p.astype(BF16)
-            ).astype(BF16)
-            dq[which, hp] = dot(ds, k)
+            dq[which, hp] = dot(dsv[hp, :, :count], k)
 
     attend_back(3 * ROWS, 4 * ROWS, 1)
 
+    reclaim((c_up, c_dn))
     zero_block = jnp.zeros((D, ROWS), BF16)
     part[4] = zero_block
     psib[4] = zero_block
     c_ps = []
-    for e in (0, 2):
-        both = dot(wkv[...], dt[:, (3 + e) * ROWS : (5 + e) * ROWS]).astype(BF16)
-        part[e] = both[:, :ROWS]
-        part[e + 1] = both[:, ROWS:]
-        c_ps.append(push(part.at[e], psib.at[e], rsend, rrecv, e, twin))
-        c_ps.append(push(part.at[e + 1], psib.at[e + 1], rsend, rrecv, e + 1, twin))
-
-    attend_back(0, 3 * ROWS, 0, (0, 1, 2))
+    da = pl.ds(0, DHALF)
+    db = pl.ds(DHALF, DHALF)
+    first4 = pl.ds(0, 4)
+    for i, cols in enumerate((da, db)):
+        every = dot(wkv[cols, :], dt[:, 3 * ROWS : 7 * ROWS]).astype(BF16)
+        for e in range(4):
+            part[e, cols, :] = every[:, e * ROWS : (e + 1) * ROWS]
+        c_ps.append(
+            push(part.at[first4, cols], psib.at[first4, cols], rrecv, i, twin)
+        )
+
+    attend_back(0, 3 * ROWS, 0)
     for copy in c_ps:
         copy.wait_recv()
 
@@ -412,41 +442,37 @@
             + psib[slot_of(lsib, target), cols, :].astype(F32)
         )
 
-    da = pl.ds(0, DHALF)
-    db = pl.ds(DHALF, DHALF)
-
     c_x = {}
 
     def opposite_step(rr):
-        s0 = 8 + 6 * rr
+        s0 = 5 + 6 * rr
         sbuf[rr, 0] = summed(x + 2, rr, da).astype(BF16)
-        c_x[rr, 0] = push(sbuf.at[rr, 0], xo.at[rr, 0], rsend, rrecv, s0, right)
+        c_x[rr, 0] = push(sbuf.at[rr, 0], xo.at[rr, 0], rrecv, s0, right)
         sbuf[rr, 1] = summed(x + 2, rr, db).astype(BF16)
-        c_x[rr, 1] = push(sbuf.at[rr, 1], xo.at[rr, 1], rsend, rrecv, s0 + 1, left)
+        c_x[rr, 1] = push(sbuf.at[rr, 1], xo.at[rr, 1], rrecv, s0 + 1, left)
 
     def direct_step(rr):
-        s0 = 8 + 6 * rr
+        s0 = 5 + 6 * rr
         sbuf[rr, 2] = summed(x + 1, rr, db).astype(BF16)
-        c_x[rr, 2] = push(sbuf.at[rr, 2], yl.at[rr, db], rsend, rrecv, s0 + 2, right)
+        c_x[rr, 2] = push(sbuf.at[rr, 2], yl.at[rr, db], rrecv, s0 + 2, right)
         sbuf[rr, 3] = summed(x + 3, rr, da).astype(BF16)
-        c_x[rr, 3] = push(sbuf.at[rr, 3], yr.at[rr, da], rsend, rrecv, s0 + 3, left)
+        c_x[rr, 3] = push(sbuf.at[rr, 3], yr.at[rr, da], rrecv, s0 + 3, left)
 
     def second_step(rr):
-        s0 = 8 + 6 * rr
+        s0 = 5 + 6 * rr
         c_x[rr, 0].wait_recv()
         sbuf[rr, 4] = (summed(x + 1, rr, da) + xo[rr, 0].astype(F32)).astype(BF16)
-        c_x[rr, 4] = push(sbuf.at[rr, 4], yl.at[rr, da], rsend, rrecv, s0 + 4, right)
+        c_x[rr, 4] = push(sbuf.at[rr, 4], yl.at[rr, da], rrecv, s0 + 4, right)
         c_x[rr, 1].wait_recv()
         sbuf[rr, 5] = (summed(x + 3, rr, db) + xo[rr, 1].astype(F32)).astype(BF16)
-        c_x[rr, 5] = push(sbuf.at[rr, 5], yr.at[rr, db], rsend, rrecv, s0 + 5, left)
+        c_x[rr, 5] = push(sbuf.at[rr, 5], yr.at[rr, db], rrecv, s0 + 5, left)
 
     opposite_step(1)
-    attend_back(0, 3 * ROWS, 0, (3,))
     halves_t = dot(wkv[...], dt[:, 0 : 2 * ROWS]).astype(BF16)
     hsend[0] = halves_t[:, :ROWS]
     hsend[1] = halves_t[:, ROWS:]
-    c_hd = push(hsend.at[0], hrecv.at[0], rsend, rrecv, 4, down)
-    c_hu = push(hsend.at[1], hrecv.at[1], rsend, rrecv, 5, up)
+    c_hd = push(hsend.at[0], hrecv.at[0], rrecv, 2, down)
+    c_hu = push(hsend.at[1], hrecv.at[1], rrecv, 3, up)
     direct_step(1)
     second_step(1)
     opposite_step(0)
@@ -459,11 +485,11 @@
 
     for slot in (2, 3, 4, 5):
         c_x[1, slot].wait_recv()
-    for i, cols in enumerate((da, db)):
-        tbuf[i] = (
+    for cols in (da, db):
+        tbuf[cols] = (
             summed(x, 1, cols) + yl[1, cols, :].astype(F32) + yr[1, cols, :].astype(F32)
         ).astype(BF16)
-        c_x[2, i] = push(tbuf.at[i], ybuf.at[i], rsend, rrecv, 6 + i, across)
+    c_t = push(tbuf, ybuf, rrecv, 4, across)
     second_step(0)
     c_hd.wait_recv()
     c_hu.wait_recv()
@@ -474,12 +500,10 @@
     own_t = own_t + jnp.concatenate([summed(x, 0, da), summed(x, 0, db)], 0)
     grad_in = grad_in + jnp.transpose(own_t)
     unit_b, inv_b = normalize(xv[...].astype(F32))
-    c_x[2, 0].wait_recv()
-    c_x[2, 1].wait_recv()
-    grad_in = grad_in + jnp.transpose(jnp.concatenate([ybuf[0], ybuf[1]], 0).astype(F32))
+    c_t.wait_recv()
+    grad_in = grad_in + jnp.transpose(ybuf[...].astype(F32))
     gout_hbm[...] = (grad_resid + normalize_back(unit_b, inv_b, grad_in)).astype(BF16)
-    for copy in sends:
-        copy.wait_send()
+    reclaim()
 
 
 def on_device(nodes, experts_list, w_query, w_key, w_value, w_out, w_up, w_down, cotangent):
@@ -508,6 +532,9 @@
             tile(PAIRS, 128, 2 * ROWS),
             tile(PAIRS, 2 * ROWS, 128),
             tile(PAIRS, 128, 2 * ROWS),
+            tile(PAIRS, 2 * ROWS, 4 * ROWS, dtype=F32),
+            tile(PAIRS, 2 * ROWS, 4 * ROWS),
+            tile(PAIRS, 2 * ROWS, 4 * ROWS),
             tile(PAIRS, 2 * ROWS, 7 * ROWS, dtype=F32),
             tile(2, PAIRS, 2 * ROWS, 128, dtype=F32),
             tile(2, PAIRS, 2 * ROWS, 128, dtype=F32),
@@ -526,18 +553,17 @@
             tile(2, D, ROWS),
             tile(2, D, ROWS),
             tile(2, 6, DHALF, ROWS),
-            tile(2, DHALF, ROWS),
-            tile(2, DHALF, ROWS),
+            tile(D, ROWS),
+            tile(D, ROWS),
             tile(4 * ROWS, D),
             tile(ROWS, FF),
             tile(ROWS, D, dtype=F32),
             tile(ROWS, FF, dtype=F32),
             pltpu.SemaphoreType.DMA((9,)),
             pltpu.SemaphoreType.REGULAR((2,)),
+            pltpu.SemaphoreType.DMA((19,)),
             pltpu.SemaphoreType.DMA((25,)),
-            pltpu.SemaphoreType.DMA((25,)),
-            pltpu.SemaphoreType.DMA((20,)),
-            pltpu.SemaphoreType.DMA((20,)),
+            pltpu.SemaphoreType.DMA((17,)),
         ],
         compiler_params=pltpu.CompilerParams(
             collective_id=0, has_side_effects=True, vmem_limit_bytes=28 * 1024 * 1024

time: 49.1 us -> 46.5 us (0.947)
  Pallas kernels: 47 us -> 44.5 us
    pallas_call x1, Pallas kernels: 47 us -> 44.5 us  [on_device(): pl.pallas_call(kernel, out_shape=(out, out), in_specs=[pl.BlockSpec(memor...]
where the time goes in v5:
time: 46.5 us; the launch traced here: 46.4 us
  Pallas kernels  44.5 us (96%)
  local copies, waits for them, and re-layouts  1.31 us (3%)
  between operations  0.64 us (1%)
    pallas_call x1, Pallas kernels, on_device(): pl.pallas_call(kernel, out_shape=(out, out), in_specs=[pl.BlockSpec(memor...  44.5 us
    unnamed x2, local copies, waits for them, and re-layouts  1.31 us

profile of v5, /device:TPU:2, one launch (start us, length us, event | category | flops | bytes accessed | tf_op | source)
XLA Modules:
  0.0 46.4 jit_solution(2264471288278851035)
XLA Ops:
  0.6 44.5 %exphormer.1 = (bf16[128,512]{1,0:T(8,128)(2,1)S(1)}, bf16[128,512]{1,0:T(8,128)(2,1)S(1)}) custom-call(s32[1,4]{1,0:T(1,128)} %list_hbm.1, bf16[128,512]{1,0:T(8,128)(2,1)} %nodes_hbm.1, s32[1,4]{1,0:T(1,128)} %list_hbm.1, bf16[512,512]{1,0:T(8,128)(2,1)} %wq_hbm.1, bf16[512,512]{1,0:T(8,128)(2,1)} %wk_hbm.1, bf16[512,512]{1,0:T(8,128)(2,1)} %wv_hbm.1, ...), custom_call_target="tpu_custom_call" | custom-call | tf_op jit(solution)/shard_map/exphormer/pallas_call | solution.py:515
  45.1 0.7 %copy.13 = bf16[128,512]{1,0:T(8,128)(2,1)} copy(bf16[128,512]{1,0:T(8,128)(2,1)S(1)} %get-tuple-element.4) | data formatting | bytes 262144
  45.8 0.7 %copy.14 = bf16[128,512]{1,0:T(8,128)(2,1)} copy(bf16[128,512]{1,0:T(8,128)(2,1)S(1)} %get-tuple-element.5) | data formatting | bytes 262144

commit v6 on v5

--- a/solution.py
+++ b/solution.py
@@ -54,7 +54,6 @@
 
 
 def kernel(
-    listed,
     nodes_hbm,
     list_hbm,
     wq_hbm,
@@ -64,8 +63,7 @@
     wu_hbm,
     wd_hbm,
     cot_hbm,
-    out_hbm,
-    gout_hbm,
+    both_out,
     xv,
     cotv,
     wq,
@@ -94,6 +92,7 @@
     dt,
     part,
     psib,
+    listed,
     lsib,
     hsend,
     hrecv,
@@ -139,16 +138,18 @@
     def greet(peer):
         pl.semaphore_signal(barrier, inc=1, device_id=peer, device_id_type=MESH)
 
-    for peer in (right, left, across, twin):
+    greet(across)
+
+    @pl.when(z < final)
+    def _():
+        greet(up)
+
+    @pl.when(z == 0)
+    def _():
+        greet(down)
+
+    for peer in (right, left, twin):
         greet(peer)
-
-    @pl.when(z < final)
-    def _():
-        greet(up)
-
-    @pl.when(z == 0)
-    def _():
-        greet(down)
 
     pl.semaphore_wait(barrier, 4 + jnp.where(z > 0, 1, 0) + jnp.where(z == final, 1, 0))
 
@@ -206,8 +207,6 @@
     c_r[0, 0] = push(nodes_hbm.at[top], gath.at[own, top], grecv, 0, right)
     c_l[0, 1] = push(nodes_hbm.at[bottom], gath.at[own, bottom], grecv, 5, left)
     c_y.append(push(nodes_hbm.at[bottom], gath.at[own, bottom], grecv, 13, across))
-    c_r[0, 1] = push(nodes_hbm.at[bottom], gath.at[own, bottom], grecv, 1, right)
-    c_l[0, 0] = push(nodes_hbm.at[top], gath.at[own, top], grecv, 4, left)
 
     loads = []
 
@@ -222,6 +221,7 @@
     ld_wv = load(wv_hbm, wkv.at[:, pl.ds(D, D)])
     ld_wq = load(wq_hbm, wq)
     ld_own = load(nodes_hbm, gath.at[own])
+    ld_list = load(list_hbm, listed)
     ld_cot = load(cot_hbm, cotv)
     ld_wd = load(wd_hbm, wd)
     ld_wo = load(wo_hbm, wo)
@@ -261,6 +261,8 @@
     def to_twin(slot, who):
         c_tw.append(push(gath.at[who], gath.at[who], grecv, slot, twin))
 
+    c_r[0, 1] = push(nodes_hbm.at[bottom], gath.at[own, bottom], grecv, 1, right)
+    c_l[0, 0] = push(nodes_hbm.at[top], gath.at[own, top], grecv, 4, left)
     c_up = plan(nodes_hbm, halo.at[0], grecv, 14, up)
     c_dn = plan(nodes_hbm, halo.at[1], grecv, 15, down)
 
@@ -279,15 +281,11 @@
     other = block(x, 1 - h)
     c_y[0].wait_recv()
     c_r[1, 0] = push(gath.at[other, top], gath.at[other, top], grecv, 2, right)
-    c_l[1, 0] = push(gath.at[other, top], gath.at[other, top], grecv, 6, left)
     c_y[1].wait_recv()
     c_l[1, 1] = push(gath.at[other, bottom], gath.at[other, bottom], grecv, 7, left)
+    c_l[1, 0] = push(gath.at[other, top], gath.at[other, top], grecv, 6, left)
     c_r[1, 1] = push(gath.at[other, bottom], gath.at[other, bottom], grecv, 3, right)
     to_twin(17, other)
-    c_r[0, 1].wait_recv()
-    to_twin(18, block(x + 3, h))
-    c_l[0, 0].wait_recv()
-    to_twin(19, block(x + 1, h))
 
     @pl.when(z < final)
     def _():
@@ -317,6 +315,10 @@
 
     reclaim([copy for copy, _ in sends[8:]])
     forward(1)
+    c_r[0, 1].wait_recv()
+    to_twin(18, block(x + 3, h))
+    c_l[0, 0].wait_recv()
+    to_twin(19, block(x + 1, h))
     fwd_r[0].wait_recv()
     fwd_l[0].wait_recv()
     to_twin(22, block(x + 2, h))
@@ -341,6 +343,7 @@
         copy.wait_recv()
     c_list.wait_recv()
     ld_own.wait()
+    ld_list.wait()
 
     for e in range(4):
         unit_e, _ = normalize(gath[listed[0, e]].astype(F32))
@@ -481,7 +484,7 @@
     own_t = dot(wkv[...], dt[:, 2 * ROWS : 3 * ROWS])
     grad_q = jnp.concatenate([head_join(dq[0, hp] + dq[1, hp]) for hp in range(PAIRS)], 1)
     grad_in = dot_t((grad_q * 0.125).astype(BF16), wq[...])
-    out_hbm[...] = (residv[...] + dot(actv[...], wd[...])).astype(BF16)
+    both_out[:, 0:D] = residv[...] + dot(actv[...], wd[...])
 
     for slot in (2, 3, 4, 5):
         c_x[1, slot].wait_recv()
@@ -502,7 +505,7 @@
     unit_b, inv_b = normalize(xv[...].astype(F32))
     c_t.wait_recv()
     grad_in = grad_in + jnp.transpose(ybuf[...].astype(F32))
-    gout_hbm[...] = (grad_resid + normalize_back(unit_b, inv_b, grad_in)).astype(BF16)
+    both_out[:, D : 2 * D] = grad_resid + normalize_back(unit_b, inv_b, grad_in)
     reclaim()
 
 
@@ -512,11 +515,11 @@
     tile = lambda *shape, dtype=BF16: pltpu.VMEM(shape, dtype)
     out = jax.ShapeDtypeStruct((rows, width), BF16)
     vm = pl.BlockSpec(memory_space=pltpu.VMEM)
-    return pl.pallas_call(
+    both = pl.pallas_call(
         kernel,
-        out_shape=(out, out),
-        in_specs=[pl.BlockSpec(memory_space=pltpu.SMEM)] + [hbm] * 9,
-        out_specs=(vm, vm),
+        out_shape=jax.ShapeDtypeStruct((rows, 2 * width), F32),
+        in_specs=[hbm] * 9,
+        out_specs=vm,
         scratch_shapes=[
             tile(ROWS, D),
             tile(ROWS, D),
@@ -547,6 +550,7 @@
             tile(5, D, ROWS),
             tile(5, D, ROWS),
             pltpu.SMEM((1, 4), jnp.int32),
+            pltpu.SMEM((1, 4), jnp.int32),
             tile(2, D, ROWS),
             tile(2, D, ROWS),
             tile(2, 2, DHALF, ROWS),
@@ -559,7 +563,7 @@
             tile(ROWS, FF),
             tile(ROWS, D, dtype=F32),
             tile(ROWS, FF, dtype=F32),
-            pltpu.SemaphoreType.DMA((9,)),
+            pltpu.SemaphoreType.DMA((10,)),
             pltpu.SemaphoreType.REGULAR((2,)),
             pltpu.SemaphoreType.DMA((19,)),
             pltpu.SemaphoreType.DMA((25,)),
@@ -570,12 +574,12 @@
         ),
         name="exphormer",
     )(
-        experts_list,
         *(
             pltpu.with_memory_space_constraint(a, pltpu.HBM)
             for a in (nodes, experts_list, w_query, w_key, w_value, w_out, w_up, w_down, cotangent)
         ),
     )
+    return (both[:, :width].astype(BF16), both[:, width:].astype(BF16))
 
 
 def solution(mesh):

time: 46.5 us -> 45.4 us (0.976)
  Pallas kernels: 44.5 us -> 43.8 us
  local copies, waits for them, and re-layouts: 1.31 us -> 0.72 us
    unnamed x2 -> x0, local copies, waits for them, and re-layouts: 1.31 us -> none
    slice x0 -> x1, local copies, waits for them, and re-layouts: none -> 0.72 us  [on_device(): return (both[:, :width].astype(BF16), both[:, width:].astype(BF16))]
    pallas_call x1, Pallas kernels: 44.5 us -> 43.8 us  [on_device(): pl.pallas_call(kernel, out_shape=jax.ShapeDtypeStruct((rows, 2 * width),...]
where the time goes in v6:
time: 45.4 us; the launch traced here: 45.2 us
  Pallas kernels  43.8 us (96%)
  local copies, waits for them, and re-layouts  0.72 us (2%)
  between operations  0.65 us (1%)
    pallas_call x1, Pallas kernels, on_device(): pl.pallas_call(kernel, out_shape=jax.ShapeDtypeStruct((rows, 2 * width),...  43.8 us

profile of v6, /device:TPU:2, one launch (start us, length us, event | category | flops | bytes accessed | tf_op | source)
XLA Modules:
  0.0 45.2 jit_solution(5289500880166446562)
XLA Ops:
  0.6 43.8 %exphormer.1 = f32[128,1024]{1,0:T(8,128)S(1)} custom-call(bf16[128,512]{1,0:T(8,128)(2,1)} %nodes_hbm.1, s32[1,4]{1,0:T(1,128)} %list_hbm.1, bf16[512,512]{1,0:T(8,128)(2,1)} %wq_hbm.1, bf16[512,512]{1,0:T(8,128)(2,1)} %wk_hbm.1, bf16[512,512]{1,0:T(8,128)(2,1)} %wv_hbm.1, bf16[512,512]{1,0:T(8,128)(2,1)} %wo_hbm.1, bf16[512,1024]{1,0:T(8,128)(2,1)} %wu_hbm.1, ...), custom_call_target="tpu_custom_call" | custom-call | tf_op jit(solution)/shard_map/exphormer/pallas_call | solution.py:518
  44.5 0.7 %fusion = (bf16[128,512]{1,0:T(8,128)(2,1)}, bf16[128,512]{1,0:T(8,128)(2,1)}) fusion(bf16[128,1024]{1,0:T(8,128)(2,1)S(1)} %convert.4), kind=kLoop, calls=%fused_computation | loop fusion | bytes 524288 | tf_op jit(solution)/shard_map/slice | solution.py:582
  (1 shorter events, 0.0 us)

commit v7 on v6

--- a/solution.py
+++ b/solution.py
@@ -327,18 +327,18 @@
         pl.semaphore_wait(ready.at[1], 1)
         c_dn.start()
 
+    c_r[1, 1].wait_recv()
+    to_twin(20, block(x + 3, 1 - h))
+    c_l[1, 0].wait_recv()
+    to_twin(21, block(x + 1, 1 - h))
+    fwd_r[1].wait_recv()
+    fwd_l[1].wait_recv()
+    to_twin(23, block(x + 2, 1 - h))
     c_up.wait_recv()
     project(halo[0], 0)
     c_dn.wait_recv()
     project(halo[1], ROWS)
-    c_r[1, 1].wait_recv()
-    to_twin(20, block(x + 3, 1 - h))
-    c_l[1, 0].wait_recv()
-    to_twin(21, block(x + 1, 1 - h))
     attend(0, 3 * ROWS, 0)
-    fwd_r[1].wait_recv()
-    fwd_l[1].wait_recv()
-    to_twin(23, block(x + 2, 1 - h))
     for copy in c_tw:
         copy.wait_recv()
     c_list.wait_recv()
@@ -429,6 +429,11 @@
         )
 
     attend_back(0, 3 * ROWS, 0)
+    halves_t = dot(wkv[...], dt[:, 0 : 2 * ROWS]).astype(BF16)
+    hsend[0] = halves_t[:, :ROWS]
+    hsend[1] = halves_t[:, ROWS:]
+    c_hd = push(hsend.at[0], hrecv.at[0], rrecv, 2, down)
+    c_hu = push(hsend.at[1], hrecv.at[1], rrecv, 3, up)
     for copy in c_ps:
         copy.wait_recv()
 
@@ -471,20 +476,14 @@
         c_x[rr, 5] = push(sbuf.at[rr, 5], yr.at[rr, db], rrecv, s0 + 5, left)
 
     opposite_step(1)
-    halves_t = dot(wkv[...], dt[:, 0 : 2 * ROWS]).astype(BF16)
-    hsend[0] = halves_t[:, :ROWS]
-    hsend[1] = halves_t[:, ROWS:]
-    c_hd = push(hsend.at[0], hrecv.at[0], rrecv, 2, down)
-    c_hu = push(hsend.at[1], hrecv.at[1], rrecv, 3, up)
+    own_t = dot(wkv[...], dt[:, 2 * ROWS : 3 * ROWS])
+    grad_q = jnp.concatenate([head_join(dq[0, hp] + dq[1, hp]) for hp in range(PAIRS)], 1)
+    grad_in = dot_t((grad_q * 0.125).astype(BF16), wq[...])
+    both_out[:, 0:D] = residv[...] + dot(actv[...], wd[...])
     direct_step(1)
     second_step(1)
     opposite_step(0)
     direct_step(0)
-
-    own_t = dot(wkv[...], dt[:, 2 * ROWS : 3 * ROWS])
-    grad_q = jnp.concatenate([head_join(dq[0, hp] + dq[1, hp]) for hp in range(PAIRS)], 1)
-    grad_in = dot_t((grad_q * 0.125).astype(BF16), wq[...])
-    both_out[:, 0:D] = residv[...] + dot(actv[...], wd[...])
 
     for slot in (2, 3, 4, 5):
         c_x[1, slot].wait_recv()

time: 45.4 us -> 44.8 us (0.987)
  Pallas kernels: 43.8 us -> 43.3 us
    pallas_call x1, Pallas kernels: 43.8 us -> 43.3 us  [on_device(): pl.pallas_call(kernel, out_shape=jax.ShapeDtypeStruct((rows, 2 * width),...]
where the time goes in v7:
time: 44.8 us; the launch traced here: 44.7 us
  Pallas kernels  43.3 us (97%)
  local copies, waits for them, and re-layouts  0.72 us (2%)
  between operations  0.65 us (1%)
    pallas_call x1, Pallas kernels, on_device(): pl.pallas_call(kernel, out_shape=jax.ShapeDtypeStruct((rows, 2 * width),...  43.3 us

profile of v7, /device:TPU:2, one launch (start us, length us, event | category | flops | bytes accessed | tf_op | source)
XLA Modules:
  0.0 44.7 jit_solution(11018658599917365071)
XLA Ops:
  0.6 43.3 %exphormer.1 = f32[128,1024]{1,0:T(8,128)S(1)} custom-call(bf16[128,512]{1,0:T(8,128)(2,1)} %nodes_hbm.1, s32[1,4]{1,0:T(1,128)} %list_hbm.1, bf16[512,512]{1,0:T(8,128)(2,1)} %wq_hbm.1, bf16[512,512]{1,0:T(8,128)(2,1)} %wk_hbm.1, bf16[512,512]{1,0:T(8,128)(2,1)} %wv_hbm.1, bf16[512,512]{1,0:T(8,128)(2,1)} %wo_hbm.1, bf16[512,1024]{1,0:T(8,128)(2,1)} %wu_hbm.1, ...), custom_call_target="tpu_custom_call" | custom-call | tf_op jit(solution)/shard_map/exphormer/pallas_call | solution.py:517
  44.0 0.7 %fusion = (bf16[128,512]{1,0:T(8,128)(2,1)}, bf16[128,512]{1,0:T(8,128)(2,1)}) fusion(bf16[128,1024]{1,0:T(8,128)(2,1)S(1)} %convert.4), kind=kLoop, calls=%fused_computation | loop fusion | bytes 524288 | tf_op jit(solution)/shard_map/slice | solution.py:581
  (1 shorter events, 0.0 us)

commit v8 on v7

--- a/solution.py
+++ b/solution.py
@@ -102,6 +102,8 @@
     sbuf,
     tbuf,
     ybuf,
+    wot,
+    wut,
     nbuf,
     actv,
     residv,
@@ -313,6 +315,10 @@
             v = kv[base : base + count, D + hp * 128 : D + (hp + 1) * 128]
             oacc[which, hp] = dot(wexp[hp, :, base : base + count].astype(BF16), v)
 
+    ld_wo.wait()
+    ld_wu.wait()
+    wot[...] = jnp.transpose(wo[...])
+    wut[...] = jnp.transpose(wu[...])
     reclaim([copy for copy, _ in sends[8:]])
     forward(1)
     c_r[0, 1].wait_recv()
@@ -362,11 +368,9 @@
         o = oacc[0, hp] * f0 + oacc[1, hp] * f1
         mixv[:, hp * 128 : (hp + 1) * 128] = head_join(o).astype(BF16)
 
-    ld_wo.wait()
     mixed = mixv[...]
     resid = xv[...].astype(F32) + dot(mixed, wo[...])
     unit2, inv_std2 = normalize(resid)
-    ld_wu.wait()
     pre = dot(unit2.astype(BF16), wu[...])
     cot = cotv[...]
     c0 = 0.7978845608028654
@@ -377,9 +381,9 @@
     actv[...] = act.astype(BF16)
     residv[...] = resid
     grad_pre = (gact[...] * slope).astype(BF16)
-    grad_norm2 = dot_t(grad_pre, wu[...])
+    grad_norm2 = dot(grad_pre, wut[...])
     grad_resid = cot.astype(F32) + normalize_back(unit2, inv_std2, grad_norm2)
-    grad_mixed = dot_t(grad_resid.astype(BF16), wo[...]).astype(BF16)
+    grad_mixed = dot(grad_resid.astype(BF16), wot[...]).astype(BF16)
     for hp in range(PAIRS):
         stacked = head_stack(grad_mixed[:, hp * 128 : (hp + 1) * 128])
         g2[hp] = stacked
@@ -558,6 +562,8 @@
             tile(2, 6, DHALF, ROWS),
             tile(D, ROWS),
             tile(D, ROWS),
+            tile(D, D),
+            tile(FF, D),
             tile(4 * ROWS, D),
             tile(ROWS, FF),
             tile(ROWS, D, dtype=F32),

time: 44.8 us -> 44.5 us (level)
  no operation moved by 1% of the time
where the time goes in v8:
time: 44.5 us; the launch traced here: 44.4 us
  Pallas kernels  43 us (97%)
  local copies, waits for them, and re-layouts  0.72 us (2%)
  between operations  0.65 us (1%)
    pallas_call x1, Pallas kernels, on_device(): pl.pallas_call(kernel, out_shape=jax.ShapeDtypeStruct((rows, 2 * width),...  43 us

profile of v8, /device:TPU:2, one launch (start us, length us, event | category | flops | bytes accessed | tf_op | source)
XLA Modules:
  0.0 44.4 jit_solution(11939600814568833113)
XLA Ops:
  0.6 43.0 %exphormer.1 = f32[128,1024]{1,0:T(8,128)S(1)} custom-call(bf16[128,512]{1,0:T(8,128)(2,1)} %nodes_hbm.1, s32[1,4]{1,0:T(1,128)} %list_hbm.1, bf16[512,512]{1,0:T(8,128)(2,1)} %wq_hbm.1, bf16[512,512]{1,0:T(8,128)(2,1)} %wk_hbm.1, bf16[512,512]{1,0:T(8,128)(2,1)} %wv_hbm.1, bf16[512,512]{1,0:T(8,128)(2,1)} %wo_hbm.1, bf16[512,1024]{1,0:T(8,128)(2,1)} %wu_hbm.1, ...), custom_call_target="tpu_custom_call" | custom-call | tf_op jit(solution)/shard_map/exphormer/pallas_call | solution.py:521
  43.7 0.7 %fusion = (bf16[128,512]{1,0:T(8,128)(2,1)}, bf16[128,512]{1,0:T(8,128)(2,1)}) fusion(bf16[128,1024]{1,0:T(8,128)(2,1)S(1)} %convert.4), kind=kLoop, calls=%fused_computation | loop fusion | bytes 524288 | tf_op jit(solution)/shard_map/slice | solution.py:587
  (1 shorter events, 0.0 us)

commit v9 on v8

--- a/solution.py
+++ b/solution.py
@@ -165,7 +165,7 @@
 
     sends = []
 
-    pool = list(range(19))
+    pool = list(range(20))
 
     def plan(src, dst, rsems, slot, peer):
         index = pool.pop(0)
@@ -489,13 +489,14 @@
     opposite_step(0)
     direct_step(0)
 
-    for slot in (2, 3, 4, 5):
-        c_x[1, slot].wait_recv()
-    for cols in (da, db):
+    c_t = []
+    for cols, slots, place in ((da, (3, 4), 4), (db, (2, 5), 17)):
+        for slot in slots:
+            c_x[1, slot].wait_recv()
         tbuf[cols] = (
             summed(x, 1, cols) + yl[1, cols, :].astype(F32) + yr[1, cols, :].astype(F32)
         ).astype(BF16)
-    c_t = push(tbuf, ybuf, rrecv, 4, across)
+        c_t.append(push(tbuf.at[cols], ybuf.at[cols], rrecv, place, across))
     second_step(0)
     c_hd.wait_recv()
     c_hu.wait_recv()
@@ -506,7 +507,8 @@
     own_t = own_t + jnp.concatenate([summed(x, 0, da), summed(x, 0, db)], 0)
     grad_in = grad_in + jnp.transpose(own_t)
     unit_b, inv_b = normalize(xv[...].astype(F32))
-    c_t.wait_recv()
+    for copy in c_t:
+        copy.wait_recv()
     grad_in = grad_in + jnp.transpose(ybuf[...].astype(F32))
     both_out[:, D : 2 * D] = grad_resid + normalize_back(unit_b, inv_b, grad_in)
     reclaim()
@@ -570,9 +572,9 @@
             tile(ROWS, FF, dtype=F32),
             pltpu.SemaphoreType.DMA((10,)),
             pltpu.SemaphoreType.REGULAR((2,)),
-            pltpu.SemaphoreType.DMA((19,)),
+            pltpu.SemaphoreType.DMA((20,)),
             pltpu.SemaphoreType.DMA((25,)),
-            pltpu.SemaphoreType.DMA((17,)),
+            pltpu.SemaphoreType.DMA((18,)),
         ],
         compiler_params=pltpu.CompilerParams(
             collective_id=0, has_side_effects=True, vmem_limit_bytes=28 * 1024 * 1024

time: 44.5 us -> 44.5 us (level)
  no operation moved by 1% of the time
where the time goes in v9:
time: 44.5 us; the launch traced here: 44.4 us
  Pallas kernels  43 us (97%)
  local copies, waits for them, and re-layouts  0.72 us (2%)
  between operations  0.65 us (1%)
    pallas_call x1, Pallas kernels, on_device(): pl.pallas_call(kernel, out_shape=jax.ShapeDtypeStruct((rows, 2 * width),...  43 us

profile of v9, /device:TPU:2, one launch (start us, length us, event | category | flops | bytes accessed | tf_op | source)
XLA Modules:
  0.0 44.4 jit_solution(16508220274439251998)
XLA Ops:
  0.6 43.0 %exphormer.1 = f32[128,1024]{1,0:T(8,128)S(1)} custom-call(bf16[128,512]{1,0:T(8,128)(2,1)} %nodes_hbm.1, s32[1,4]{1,0:T(1,128)} %list_hbm.1, bf16[512,512]{1,0:T(8,128)(2,1)} %wq_hbm.1, bf16[512,512]{1,0:T(8,128)(2,1)} %wk_hbm.1, bf16[512,512]{1,0:T(8,128)(2,1)} %wv_hbm.1, bf16[512,512]{1,0:T(8,128)(2,1)} %wo_hbm.1, bf16[512,1024]{1,0:T(8,128)(2,1)} %wu_hbm.1, ...), custom_call_target="tpu_custom_call" | custom-call | tf_op jit(solution)/shard_map/exphormer/pallas_call | solution.py:523
  43.7 0.7 %fusion = (bf16[128,512]{1,0:T(8,128)(2,1)}, bf16[128,512]{1,0:T(8,128)(2,1)}) fusion(bf16[128,1024]{1,0:T(8,128)(2,1)S(1)} %convert.4), kind=kLoop, calls=%fused_computation | loop fusion | bytes 524288 | tf_op jit(solution)/shard_map/slice | solution.py:589
  (1 shorter events, 0.0 us)
